TPU v7x, 128 devices: a whole 4x4x4 slice. The times are simulated.
128 devices in a mesh: grp: 4 (over z_lo, core), dev: 32 (over y, z_hi, x).
Axes of the slice: x: 4, y: 4, z: 4 (z_hi: 2, z_lo: 2; z = z_hi * 2 + z_lo), core: 2. Of those that a mesh axis runs over, the one named last changes fastest.
Arguments:
- tokens: bfloat16 [16384, 2048], P(('grp', 'dev')), may hold values from -6 to 6
- queries: bfloat16 [16384, 2048], P(('grp', 'dev')), may hold values from -7.5 to 7.5
- suffix_keys: bfloat16 [16384, 2048], P(('grp', 'dev')), may hold values from -6 to 6
- suffix_values: bfloat16 [16384, 2048], P(('grp', 'dev')), may hold values from -6 to 6
- prefix_keys: bfloat16 [4, 1024, 2048], P('grp', 'dev'), may hold values from -6 to 6
- prefix_values: bfloat16 [4, 1024, 2048], P('grp', 'dev'), may hold values from -6 to 6
- out_weight: bfloat16 [2048, 2048], replicated, may hold values from -0.125 to 0.125
- norm_gain: float32 [2048], replicated, may hold values from 0.1 to 1.9
- routes: int32 [16384, 6], P(('grp', 'dev')), may hold values from 0 to 63, all different within a row; in each aligned block of 128 rows (0 to 127, 128 to 255, ...) at most 16 rows name the same one
- route_weights: float32 [16384, 6], P(('grp', 'dev')), may hold values from 0.05 to 0.5
- gate_up_weight: bfloat16 [128, 2048, 1408], P(('grp', 'dev')), may hold values from -0.125 to 0.125
- down_weight: bfloat16 [128, 704, 2048], P(('grp', 'dev')), may hold values from -0.15625 to 0.15625
Outputs:
- attended: bfloat16 [16384, 2048], P(('grp', 'dev'))
- routed: bfloat16 [16384, 2048], P(('grp', 'dev'))
Inputs may be any that keep to these rules, and one draw needn't show every extreme that they name: `routes`: each row names 6 different experts. Within the rows of one request (aligned blocks of 128 rows) no expert is named by more than 16 rows, and in some block one expert is named exactly 16 times.
All inputs are finite; a program needn't handle non-finite values.
Results may differ from a plain program's by a relative error of at most 0.019.
Values may be sent and summed in bfloat16 or wider, within the bound.
A program may use at most 128 MiB of HBM per device.

v0:
```python
import math

import jax
import jax.numpy as jnp
from jax import lax
from jax.sharding import PartitionSpec as P

HEADS = 16
HEAD_DIM = 128
TOP = 6


def half_expert(rows, gate_up, down_proj):
    hidden_units = down_proj.shape[0]
    projected = jnp.dot(rows, gate_up, preferred_element_type=jnp.float32)
    active = (jax.nn.silu(projected[:, :hidden_units]) * projected[:, hidden_units:]).astype(
        jnp.bfloat16
    )
    return jnp.dot(active, down_proj, preferred_element_type=jnp.float32).astype(jnp.bfloat16)


def on_device(
    tokens,
    queries,
    suffix_keys,
    suffix_values,
    prefix_keys,
    prefix_values,
    out_weight,
    norm_gain,
    routes,
    route_weights,
    gate_up_weight,
    down_weight,
):
    rows_here = tokens.shape[0]
    width = tokens.shape[1]
    divisor = math.sqrt(HEAD_DIM)
    query_heads = queries.reshape(rows_here, HEADS, HEAD_DIM)
    running_max = jnp.full((HEADS, rows_here), -jnp.inf, jnp.float32)
    denominator = jnp.zeros((HEADS, rows_here), jnp.float32)
    weighted = jnp.zeros((HEADS, rows_here, HEAD_DIM), jnp.float32)
    key_piece = lax.all_gather(prefix_keys[0], "dev", axis=0, tiled=True).reshape(
        -1, HEADS, HEAD_DIM
    )
    value_piece = lax.all_gather(prefix_values[0], "dev", axis=0, tiled=True).reshape(
        -1, HEADS, HEAD_DIM
    )
    scores = (
        jnp.einsum("rhd,khd->hrk", query_heads, key_piece, preferred_element_type=jnp.float32)
        / divisor
    )
    new_max = jnp.max(scores, axis=-1)
    shifted = jnp.exp(scores - new_max[..., None])
    factor = jnp.exp(running_max - new_max)
    denominator = denominator * factor + jnp.sum(shifted, axis=-1)
    weighted = weighted * factor[..., None] + jnp.einsum(
        "hrk,khd->hrd",
        shifted.astype(jnp.bfloat16),
        value_piece,
        preferred_element_type=jnp.float32,
    )
    causal = jnp.arange(rows_here)[:, None] >= jnp.arange(rows_here)[None, :]
    suffix_scores = (
        jnp.einsum(
            "rhd,khd->hrk",
            query_heads,
            suffix_keys.reshape(rows_here, HEADS, HEAD_DIM),
            preferred_element_type=jnp.float32,
        )
        / divisor
    )
    suffix_scores = jnp.where(causal[None], suffix_scores, -jnp.inf)
    suffix_max = jnp.max(suffix_scores, axis=-1)
    suffix_exp = jnp.exp(suffix_scores - suffix_max[..., None])
    suffix_sum = jnp.sum(suffix_exp, axis=-1)
    suffix_acc = jnp.einsum(
        "hrk,khd->hrd",
        suffix_exp.astype(jnp.bfloat16),
        suffix_values.reshape(rows_here, HEADS, HEAD_DIM),
        preferred_element_type=jnp.float32,
    )
    merged_max = jnp.maximum(new_max, suffix_max)
    prefix_scale = jnp.exp(new_max - merged_max)
    suffix_scale = jnp.exp(suffix_max - merged_max)
    mixed = (weighted * prefix_scale[..., None] + suffix_acc * suffix_scale[..., None]) / (
        denominator * prefix_scale + suffix_sum * suffix_scale
    )[..., None]
    heads_out = jnp.transpose(mixed, (1, 0, 2)).reshape(rows_here, width).astype(jnp.bfloat16)
    attended = jnp.dot(heads_out, out_weight, preferred_element_type=jnp.float32).astype(
        jnp.bfloat16
    )
    residual = tokens.astype(jnp.float32) + attended.astype(jnp.float32)
    mean_square = jnp.mean(residual * residual, axis=-1, keepdims=True)
    normed = (residual * lax.rsqrt(mean_square + 1e-06) * norm_gain).astype(jnp.bfloat16)
    groups = lax.axis_size("grp")
    members = lax.axis_size("dev")
    experts = groups * members // 2
    capacity = 4 * rows_here * TOP // (3 * experts)
    flat_routes = routes.reshape(-1)
    onehot = (flat_routes[:, None] == jnp.arange(experts, dtype=jnp.int32)[None, :]).astype(
        jnp.int32
    )
    ranking = jnp.sum(jnp.cumsum(onehot, axis=0) * onehot, axis=1) - 1
    slots = flat_routes * capacity + ranking
    owners = jnp.arange(rows_here * TOP, dtype=jnp.int32) // TOP
    outgoing = jnp.zeros((experts * capacity, width), jnp.bfloat16).at[slots].set(normed[owners])
    buffer = jnp.broadcast_to(
        outgoing.reshape(experts, 1, capacity, width), (experts, 2, capacity, width)
    ).reshape(2 * experts, capacity, width)
    received = lax.all_to_all(buffer, ("grp", "dev"), split_axis=0, concat_axis=0, tiled=True)
    partial_rows = half_expert(
        received.reshape(-1, width), gate_up_weight[0], down_weight[0]
    ).reshape(2 * experts, capacity, width)
    returned = lax.all_to_all(partial_rows, ("grp", "dev"), split_axis=0, concat_axis=0, tiled=True)
    halves = returned.reshape(experts, 2, capacity, width)
    expert_table = lax.optimization_barrier(
        (halves[:, 0].astype(jnp.float32) + halves[:, 1].astype(jnp.float32)).astype(jnp.bfloat16)
    ).reshape(experts * capacity, width)
    picked = expert_table[slots].astype(jnp.float32)
    weighted_rows = picked * route_weights.reshape(-1)[:, None]
    routed = jnp.sum(weighted_rows.reshape(rows_here, TOP, width), axis=1).astype(jnp.bfloat16)
    return (attended, routed)


def solution(mesh):
    return jax.shard_map(
        on_device,
        mesh=mesh,
        in_specs=(
            P(("grp", "dev"), None),
            P(("grp", "dev"), None),
            P(("grp", "dev"), None),
            P(("grp", "dev"), None),
            P("grp", "dev", None),
            P("grp", "dev", None),
            P(),
            P(),
            P(("grp", "dev"), None),
            P(("grp", "dev"), None),
            P(("grp", "dev"), None, None),
            P(("grp", "dev"), None, None),
        ),
        out_specs=(P(("grp", "dev"), None), P(("grp", "dev"), None)),
        check_vma=False,
    )
```

profile of v0, /device:TPU:1, one launch (start us, length us, event | category | flops | bytes accessed | tf_op | source)
XLA Modules:
  0.0 513.5 jit_solution(7477060815687853919)
XLA Ops:
  9.7 2.0 copy.55
  11.8 1.8 reduce-window.6
  15.1 1.8 fusion.56
  16.9 1.0 copy-done.4
  18.0 77.1 %all-gather.5.cloned.1.call-done = bf16[1,1024,2048]{2,1,0:T(8,128)(2,1)} async-done(((bf16[1,32,2048]{2,1,0:T(8,128)(2,1)}), bf16[1,1024,2048]{2,1,0:T(8,128)(2,1)}) %all-gather.5.cloned.1.call-update) | async-done | bytes 4194320 | tf_op jit(solution)/shard_map/all_gather | solution.py:43
  95.2 6.4 %copy.38 = bf16[1,1024,2048]{1,2,0:T(8,128)(2,1)} copy(bf16[1,1024,2048]{2,1,0:T(8,128)(2,1)} %all-gather.5.cloned.1.call-done) | data formatting | bytes 8388608 | tf_op jit(solution)/shard_map/all_gather | solution.py:43
  101.6 3.5 multiply_reduce_fusion.1
  105.1 3.2 copy-done.1
  108.3 1.8 fusion
  110.1 67.4 %all-gather.7.cloned.1.call-done = bf16[1,1024,2048]{2,1,0:T(8,128)(2,1)} async-done(((bf16[1,32,2048]{2,1,0:T(8,128)(2,1)}), bf16[1,1024,2048]{2,1,0:T(8,128)(2,1)}) %all-gather.7.cloned.1.call-update) | async-done | bytes 4194320 | tf_op jit(solution)/shard_map/all_gather | solution.py:46
  177.5 6.4 %copy.41 = bf16[1,1024,2048]{1,2,0:T(8,128)(2,1)} copy(bf16[1,1024,2048]{2,1,0:T(8,128)(2,1)} %all-gather.7.cloned.1.call-done) | data formatting | bytes 8388608 | tf_op jit(solution)/shard_map/all_gather | solution.py:46
  184.0 6.9 %fusion.26 = f32[128,16,128]{0,2,1:T(8,128)S(1)} fusion(bf16[1024,16,128]{0,2,1:T(8,128)(2,1)} %bitcast.121, f32[16,128,1024]{2,1,0:T(8,128)} %copy-done.1, f32[16,128]{1,0:T(8,128)S(1)} %get-tuple-element.6, f32[128,16]{0,1:T(8,128)S(1)} %get-tuple-element.4, f32[128,16]{0,1:T(8,128)S(1)} %get-tuple-element.5), kind=kOutput, calls=%fused_computation.34 | convolution fusion | flops 543686656 | bytes 13656064 | tf_op jit(solution)/shard_map/hrk,khd->hrd/dot_general | solution.py:57
  191.6 1.4 multiply_reduce_fusion.2
  194.0 23.5 %scatter_custom_fusion = bf16[1024,2048]{1,0:T(8,128)(2,1)} fusion(s32[768]{0:T(1024)S(1)} %fusion.50, bf16[128,2048]{1,0:T(8,128)(2,1)S(1)} %multiply_convert_fusion, s32[1024]{0:T(1024)S(1)} %pad_clamp_fusion.1, bf16[]{:T(256)} %constant.17.clone.1), kind=kCustom, calls=%fused_computation.20 | custom fusion | bytes 4194306 | tf_op jit(solution)/shard_map/scatter | solution.py:107
  217.5 6.8 %broadcast_in_dim.28 = bf16[64,2,16,2048]{3,2,1,0:T(8,128)(2,1)} broadcast(bf16[64,16,2048]{2,1,0:T(8,128)(2,1)} %bitcast.120), dimensions={0,2,3} | broadcast | bytes 12582912 | tf_op jit(solution)/shard_map/broadcast_in_dim | solution.py:108
  224.3 105.2 %all_to_all.10 = bf16[128,16,2048]{2,1,0:T(8,128)(2,1)S(1)} all-to-all(bf16[128,16,2048]{2,1,0:T(8,128)(2,1)} %bitcast.117), channel_id=1, replica_groups=mesh['grp'=4,'dev'=32] {'grp','dev'}, dimensions={0} | all-to-all | bytes 16777216 | tf_op jit(solution)/shard_map/all_to_all | solution.py:111
  329.5 17.8 %fusion.3 = f32[2048,1408]{0,1:T(8,128)} fusion(bf16[2048,2048]{1,0:T(8,128)(2,1)S(1)} %bitcast.124, bf16[1,2048,1408]{2,1,0:T(8,128)(2,1)} %param.22), kind=kOutput, calls=%fused_computation.12 | convolution fusion | flops 11811160064 | bytes 25690112 | tf_op jit(solution)/shard_map/dot_general | solution.py:15
  347.3 13.5 %convolution_convert_fusion = bf16[2048,2048]{1,0:T(8,128)(2,1)} fusion(f32[2048,1408]{0,1:T(8,128)} %fusion.3, bf16[1,704,2048]{2,1,0:T(8,128)(2,1)S(1)} %copy-done), kind=kOutput, calls=%fused_computation.7 | convolution fusion | flops 5918425088 | bytes 22806528 | tf_op jit(solution)/shard_map/dot_general | solution.py:19
  360.8 7.9 %all-to-all-start.1 = ((bf16[128,16,2048]{2,1,0:T(8,128)(2,1)}), bf16[128,16,2048]{2,1,0:T(8,128)(2,1)}, u32[]{:S(2)}, u32[]{:S(2)}) async-start(bf16[128,16,2048]{2,1,0:T(8,128)(2,1)} %bitcast.123), calls=%async_computation.1 | async-start | bytes 16777216 | tf_op jit(solution)/shard_map/all_to_all | solution.py:115
  368.8 108.1 %all-to-all-done.1 = bf16[128,16,2048]{2,1,0:T(8,128)(2,1)} async-done(((bf16[128,16,2048]{2,1,0:T(8,128)(2,1)}), bf16[128,16,2048]{2,1,0:T(8,128)(2,1)}, u32[]{:S(2)}, u32[]{:S(2)}) %all-to-all-start.1) | async-done | bytes 8388640 | tf_op jit(solution)/shard_map/all_to_all | solution.py:115
  477.0 5.7 %fusion.7 = bf16[64,16,2048]{2,1,0:T(8,128)(2,1)} fusion(bf16[64,2,16,2048]{3,2,1,0:T(8,128)(2,1)} %bitcast.17), kind=kLoop, calls=%fused_computation.15 | loop fusion | flops 8388608 | bytes 12582912 | tf_op jit(solution)/shard_map/convert_element_type | solution.py:118
  482.7 9.8 %gather_fusion = bf16[768,2048]{1,0:T(8,128)(2,1)} fusion(bf16[1024,2048]{1,0:T(8,128)(2,1)} %bitcast.116, s32[1024]{0:T(1024)S(1)} %pad_clamp_fusion), kind=kCustom, calls=%fused_computation.1 | custom fusion | bytes 6294528 | tf_op jit(solution)/shard_map/gather | solution.py:120
  492.5 6.6 %reshape.210 = f32[128,6,2048]{2,1,0:T(8,128)} reshape(bf16[768,2048]{1,0:T(8,128)(2,1)} %gather_fusion) | data formatting | bytes 9437184 | tf_op jit(solution)/shard_map/convert_element_type | solution.py:120
  499.1 7.4 %multiply_reduce_fusion = bf16[128,2048]{1,0:T(8,128)(2,1)} fusion(f32[128,6,2048]{2,1,0:T(8,128)} %reshape.210, f32[128,6]{1,0:T(8,128)S(1)} %copy.52), kind=kLoop, calls=%fused_computation.3 | loop fusion | flops 2883584 | bytes 6818816 | tf_op jit(solution)/shard_map/reduce_sum | solution.py:122
  (49 shorter events, 6.0 us)
Async XLA Ops:
  7.2 340.1 %copy-start = (bf16[1,704,2048]{2,1,0:T(8,128)(2,1)S(1)}, bf16[1,704,2048]{2,1,0:T(8,128)(2,1)}, u32[]{:S(2)}) copy-start(bf16[1,704,2048]{2,1,0:T(8,128)(2,1)} %param.23) | copy-start | bytes 8650756
  7.2 88.0 %all-gather.5.cloned.1.call-start = ((), (), s32[]{:S(2)}) async-start(), calls=%async_computation.2 | async-start | bytes 4325376 | tf_op jit(solution)/shard_map/all_gather | solution.py:43
  7.9 169.6 %all-gather.7.cloned.1.call-start = ((), (), s32[]{:S(2)}) async-start(), calls=%async_computation.3 | async-start | bytes 4325376 | tf_op jit(solution)/shard_map/all_gather | solution.py:46
  15.1 86.5 %copy-start.6 = (bf16[128,2048]{1,0:T(8,128)(2,1)S(1)}, bf16[128,2048]{1,0:T(8,128)(2,1)}, u32[]{:S(2)}) copy-start(bf16[128,2048]{1,0:T(8,128)(2,1)} %param.13) | copy-start | bytes 1572868
  16.9 1.0 copy-start.4
  105.1 3.2 copy-start.1
  183.9 7.3 %slice-start = ((s8[8388608]{0:T(1024)(128)(4,1)}), s8[4194304]{0:T(1024)(128)(4,1)S(1)}, s32[]{:S(2)}) async-start(s8[8388608]{0:T(1024)(128)(4,1)} %bitcast.118), calls=%async_computation.4 | async-start | bytes 8388608
  183.9 7.0 %copy-start.5 = (f32[16,128,128]{1,2,0:T(8,128)S(1)}, f32[16,128,128]{1,2,0:T(8,128)}, u32[]{:S(2)}) copy-start(f32[16,128,128]{1,2,0:T(8,128)} %copy-done.4) | copy-start | bytes 3145732
  183.9 7.0 %copy-start.7 = (bf16[128,2048]{0,1:T(8,128)(2,1)S(1)}, bf16[128,2048]{0,1:T(8,128)(2,1)}, u32[]{:S(2)}) copy-start(bf16[128,2048]{0,1:T(8,128)(2,1)} %copy.55) | copy-start | bytes 1572868
  183.9 7.7 %slice-start.1 = ((s8[8388608]{0:T(1024)(128)(4,1)}), s8[4194304]{0:T(1024)(128)(4,1)S(1)}, s32[]{:S(2)}) async-start(s8[8388608]{0:T(1024)(128)(4,1)} %bitcast.118), calls=%async_computation.5 | async-start | bytes 8388608
  183.9 7.6 %copy-start.2 = (bf16[128,2048]{1,0:T(8,128)(2,1)S(1)}, bf16[128,2048]{1,0:T(8,128)(2,1)}, u32[]{:S(2)}) copy-start(bf16[128,2048]{1,0:T(8,128)(2,1)} %param.12) | copy-start | bytes 1572868
  191.6 2.2 copy-start.8
  193.0 0.8 copy-start.3
  360.8 7.9 %copy-start.9 = (f32[128,6]{0,1:T(8,128)S(1)}, f32[128,6]{0,1:T(8,128)}, u32[]{:S(2)}) copy-start(f32[128,6]{0,1:T(8,128)} %param.21) | copy-start | bytes 9220
  360.8 116.2 %all-to-all-start.1 = ((bf16[128,16,2048]{2,1,0:T(8,128)(2,1)}), bf16[128,16,2048]{2,1,0:T(8,128)(2,1)}, u32[]{:S(2)}, u32[]{:S(2)}) async-start(bf16[128,16,2048]{2,1,0:T(8,128)(2,1)} %bitcast.123), calls=%async_computation.1 | async-start | bytes 16777216 | tf_op jit(solution)/shard_map/all_to_all | solution.py:115
Sparse Core Ops, SparseCore 0:
  11.0 84.1 all-gather.4
  98.2 79.3 all-gather.6
where the time goes:
time: 521 us; the launch traced here: 514 us
  waiting for transfers between devices  254 us (49%)
  blocking collectives  105 us (20%)
  local copies, waits for them, and re-layouts  68.5 us (13%)
  matrix products  45.2 us (9%)
  other arithmetic  18 us (3%)
  between operations  14.5 us (3%)
  starting transfers between devices  7.99 us (2%)
    all_to_all x1, waiting for transfers between devices, on_device(): lax.all_to_all(partial_rows, ('grp', 'dev'), split_axis=0, concat_axis=0,...  108 us
    all_to_all x1, blocking collectives, on_device(): lax.all_to_all(buffer, ('grp', 'dev'), split_axis=0, concat_axis=0, tiled...  105 us
    all_gather x1, waiting for transfers between devices, on_device(): lax.all_gather(prefix_keys[0], 'dev', axis=0, tiled=True)  77.1 us
    all_gather x1, waiting for transfers between devices, on_device(): lax.all_gather(prefix_values[0], 'dev', axis=0, tiled=True)  67.4 us
    scatter x1, local copies, waits for them, and re-layouts, on_device(): jnp.zeros((experts * capacity, width), jnp.bfloat16).at[slots]  23.5 us
    dot_general x1, matrix products, half_expert(): projected = jnp.dot(rows, gate_up, preferred_element_type=jnp.float32)  17.8 us
    dot_general x1, matrix products, half_expert(): jnp.dot(active, down_proj, preferred_element_type=jnp.float32)  13.5 us
  transfers between devices with their start and end apart: 3, of which 3 were waited for; matrix products, arithmetic and copies ran while one was open for 4% of the time, Pallas kernels for 0%

commit v1 on v0

v1 whole, which is shorter than its diff:
```python
import functools
import math

import jax
import jax.numpy as jnp
from jax import lax
from jax.experimental import pallas as pl
from jax.experimental.pallas import tpu as pltpu
from jax.sharding import PartitionSpec as P

HEADS = 16
HEAD_DIM = 128
TOP = 6
MESH = pl.DeviceIdType.MESH
F32 = jnp.float32
BF16 = jnp.bfloat16
NT = (((1,), (1,)), ((), ()))


def attention_kernel(
    q_ref, k_ref, v_ref, sk_ref, sv_ref, tok_ref, gain_ref, ow_hbm,
    attended_ref, normed_ref,
    qbuf, kbuf, vbuf, osend, orecv, stsend, strecv, suf_acc, suf_stat, vt, hout, resid, ow,
    recv_sem, send_sem, ow_sem,
):
    me = lax.axis_index("dev")
    y, zh, x = me // 8, (me // 4) % 2, me % 4
    head = y * 4 + x
    scale = 1.0 / math.sqrt(HEAD_DIM)

    ow_copy = pltpu.make_async_copy(ow_hbm, ow, ow_sem)
    ow_copy.start()

    barrier = pltpu.get_barrier_semaphore()

    def greet(j, c):
        pl.semaphore_signal(barrier, inc=1, device_id={"dev": (me + j) % 32}, device_id_type=MESH)
        return c

    lax.fori_loop(1, 32, greet, 0)
    pl.semaphore_wait(barrier, 31)

    def columns(h):
        return pl.ds(pl.multiple_of(h * HEAD_DIM, HEAD_DIM), HEAD_DIM)

    def key_rows(d):
        return pl.ds(pl.multiple_of(d * 32, 32), 32)

    pltpu.make_async_copy(q_ref.at[:, columns(head)], qbuf.at[head], recv_sem.at[0]).start()
    pltpu.make_async_copy(k_ref.at[:, columns(head)], kbuf.at[key_rows(me), :], recv_sem.at[1]).start()
    pltpu.make_async_copy(v_ref.at[:, columns(head)], vbuf.at[key_rows(me), :], recv_sem.at[2]).start()

    def send_kv(j, c):
        dz, dy, dx = j // 16, (j // 4) % 4, j % 4
        ty, tz, tx = (y + dy) % 4, (zh + dz) % 2, (x + dx) % 4
        to = {"dev": ty * 8 + tz * 4 + tx}
        h = ty * 4 + tx
        pltpu.make_async_remote_copy(
            k_ref.at[:, columns(h)], kbuf.at[key_rows(me), :], send_sem.at[1], recv_sem.at[1],
            device_id=to, device_id_type=MESH,
        ).start()
        pltpu.make_async_remote_copy(
            v_ref.at[:, columns(h)], vbuf.at[key_rows(me), :], send_sem.at[2], recv_sem.at[2],
            device_id=to, device_id_type=MESH,
        ).start()
        return c

    def send_q(j, c):
        ty, tx = (y + j // 4) % 4, (x + j % 4) % 4
        h = ty * 4 + tx
        pltpu.make_async_remote_copy(
            q_ref.at[:, columns(h)], qbuf.at[head], send_sem.at[0], recv_sem.at[0],
            device_id={"dev": ty * 8 + zh * 4 + tx}, device_id_type=MESH,
        ).start()
        return c

    lax.fori_loop(1, 32, send_kv, 0)
    lax.fori_loop(1, 16, send_q, 0)

    key_at = lax.broadcasted_iota(jnp.int32, (128, 128), 0)
    query_at = lax.broadcasted_iota(jnp.int32, (128, 128), 1)
    allowed = key_at <= query_at
    for h in range(HEADS):
        cols = slice(h * HEAD_DIM, (h + 1) * HEAD_DIM)
        s = lax.dot_general(sk_ref[:, cols], q_ref[:, cols], NT, preferred_element_type=F32) * scale
        s = jnp.where(allowed, s, -jnp.inf)
        m = jnp.max(s, axis=0, keepdims=True)
        p = jnp.exp(s - m)
        suf_stat[0, h : h + 1, :] = m
        suf_stat[1, h : h + 1, :] = jnp.sum(p, axis=0, keepdims=True)
        val_t = sv_ref[:, cols].astype(F32).T.astype(BF16)
        suf_acc[cols, :] = jnp.dot(val_t, p.astype(BF16), preferred_element_type=F32)

    pltpu.make_async_copy(kbuf, kbuf, recv_sem.at[1]).wait()
    pltpu.make_async_copy(vbuf, vbuf, recv_sem.at[2]).wait()
    vt[...] = vbuf[...].astype(F32).T.astype(BF16)
    pltpu.make_async_copy(qbuf, qbuf, recv_sem.at[0]).wait()

    def prefix(r, c):
        s = lax.dot_general(kbuf[...], qbuf[r], NT, preferred_element_type=F32) * scale
        m = jnp.max(s, axis=0, keepdims=True)
        p = jnp.exp(s - m)
        total = jnp.sum(p, axis=0, keepdims=True)
        acc = jnp.dot(vt[...], p.astype(BF16), preferred_element_type=F32)
        osend[r] = (acc / total).astype(BF16)
        stsend[r] = jnp.concatenate([m, total, jnp.zeros((6, 128), F32)], axis=0)
        return c

    lax.fori_loop(0, 16, prefix, 0)

    pltpu.make_async_copy(osend.at[head], orecv.at[head], recv_sem.at[3]).start()
    pltpu.make_async_copy(stsend.at[head], strecv.at[head], recv_sem.at[4]).start()

    def send_out(j, c):
        ty, tx = (y + j // 4) % 4, (x + j % 4) % 4
        to = {"dev": ty * 8 + zh * 4 + tx}
        pltpu.make_async_remote_copy(
            osend.at[ty * 4 + tx], orecv.at[head], send_sem.at[3], recv_sem.at[3],
            device_id=to, device_id_type=MESH,
        ).start()
        pltpu.make_async_remote_copy(
            stsend.at[ty * 4 + tx], strecv.at[head], send_sem.at[4], recv_sem.at[4],
            device_id=to, device_id_type=MESH,
        ).start()
        return c

    lax.fori_loop(1, 16, send_out, 0)
    pltpu.make_async_copy(strecv, strecv, recv_sem.at[4]).wait()
    pltpu.make_async_copy(orecv, orecv, recv_sem.at[3]).wait()

    for h in range(HEADS):
        cols = slice(h * HEAD_DIM, (h + 1) * HEAD_DIM)
        pre_m, pre_l = strecv[h, 0:1, :], strecv[h, 1:2, :]
        suf_m, suf_l = suf_stat[0, h : h + 1, :], suf_stat[1, h : h + 1, :]
        top = jnp.maximum(pre_m, suf_m)
        a = jnp.exp(pre_m - top) * pre_l
        b = jnp.exp(suf_m - top)
        mixed = (orecv[h].astype(F32) * a + suf_acc[cols, :] * b) / (a + suf_l * b)
        hout[:, cols] = mixed.T.astype(BF16)

    ow_copy.wait()
    square = jnp.zeros((128, 1), F32)
    for n in range(4):
        cols = slice(n * 512, (n + 1) * 512)
        att = jnp.dot(hout[...], ow[:, cols], preferred_element_type=F32).astype(BF16)
        attended_ref[:, cols] = att
        res = tok_ref[:, cols].astype(F32) + att.astype(F32)
        resid[:, cols] = res
        square = square + jnp.sum(res * res, axis=1, keepdims=True)
    factor = lax.rsqrt(square * (1.0 / 2048.0) + 1e-06)
    normed_ref[...] = (resid[...] * factor * gain_ref[...]).astype(BF16)

    pltpu.make_async_copy(qbuf.at[pl.ds(0, 15)], qbuf.at[pl.ds(0, 15)], send_sem.at[0]).wait()
    pltpu.make_async_copy(kbuf.at[pl.ds(0, 992), :], kbuf.at[pl.ds(0, 992), :], send_sem.at[1]).wait()
    pltpu.make_async_copy(vbuf.at[pl.ds(0, 992), :], vbuf.at[pl.ds(0, 992), :], send_sem.at[2]).wait()
    pltpu.make_async_copy(osend.at[pl.ds(0, 15)], osend.at[pl.ds(0, 15)], send_sem.at[3]).wait()
    pltpu.make_async_copy(stsend.at[pl.ds(0, 15)], stsend.at[pl.ds(0, 15)], send_sem.at[4]).wait()


def attention(q, k, v, sk, sv, tok, gain, ow):
    vmem = pl.BlockSpec(memory_space=pltpu.VMEM)
    return pl.pallas_call(
        attention_kernel,
        out_shape=(jax.ShapeDtypeStruct((128, 2048), BF16), jax.ShapeDtypeStruct((128, 2048), BF16)),
        in_specs=[vmem] * 7 + [pl.BlockSpec(memory_space=pl.ANY)],
        out_specs=(vmem, vmem),
        scratch_shapes=[
            pltpu.VMEM((16, 128, 128), BF16),
            pltpu.VMEM((1024, 128), BF16),
            pltpu.VMEM((1024, 128), BF16),
            pltpu.VMEM((16, 128, 128), BF16),
            pltpu.VMEM((16, 128, 128), BF16),
            pltpu.VMEM((16, 8, 128), F32),
            pltpu.VMEM((16, 8, 128), F32),
            pltpu.VMEM((2048, 128), F32),
            pltpu.VMEM((2, 16, 128), F32),
            pltpu.VMEM((128, 1024), BF16),
            pltpu.VMEM((128, 2048), BF16),
            pltpu.VMEM((128, 2048), F32),
            pltpu.VMEM((2048, 2048), BF16),
            pltpu.SemaphoreType.DMA((5,)),
            pltpu.SemaphoreType.DMA((5,)),
            pltpu.SemaphoreType.DMA,
        ],
        compiler_params=pltpu.CompilerParams(
            collective_id=0, has_side_effects=True, vmem_limit_bytes=48 * 1024 * 1024
        ),
        name="attention",
    )(q, k, v, sk, sv, tok, gain, ow)


def half_expert(rows, gate_up, down_proj):
    hidden_units = down_proj.shape[0]
    projected = jnp.dot(rows, gate_up, preferred_element_type=F32)
    active = (jax.nn.silu(projected[:, :hidden_units]) * projected[:, hidden_units:]).astype(BF16)
    return jnp.dot(active, down_proj, preferred_element_type=F32).astype(BF16)


def on_device(
    tokens, queries, suffix_keys, suffix_values, prefix_keys, prefix_values,
    out_weight, norm_gain, routes, route_weights, gate_up_weight, down_weight,
):
    rows_here, width = tokens.shape
    experts, capacity = 64, 16
    named = routes.T[:, None, :] == jnp.arange(experts, dtype=jnp.int32)[None, :, None]
    member = jnp.sum(named.astype(F32), axis=0)
    gate = jnp.sum(jnp.where(named, route_weights.T[:, None, :], 0.0), axis=0)
    before = (jnp.arange(rows_here)[:, None] < jnp.arange(rows_here)[None, :]).astype(BF16)
    rank = jnp.dot(member.astype(BF16), before, preferred_element_type=F32)
    position = jnp.where(member > 0, rank, -1.0)
    place = position[:, None, :] == jnp.arange(capacity, dtype=F32)[None, :, None]
    selected = place.astype(BF16).reshape(experts * capacity, rows_here)
    weights = jnp.where(place, gate[:, None, :], 0.0)
    high = weights.astype(BF16)
    low = (weights - high.astype(F32)).astype(BF16)
    both = jnp.stack([high, low])[:, :, None]
    both = jnp.broadcast_to(both, (2, experts, 2, capacity, rows_here)).reshape(2, 2 * experts * capacity, rows_here)

    attended, normed = attention(
        queries, prefix_keys[0], prefix_values[0], suffix_keys, suffix_values, tokens,
        norm_gain.reshape(1, width), out_weight,
    )
    outgoing = jnp.dot(selected, normed, preferred_element_type=F32).astype(BF16)
    buffer = jnp.broadcast_to(
        outgoing.reshape(experts, 1, capacity, width), (experts, 2, capacity, width)
    ).reshape(2 * experts, capacity, width)
    received = lax.all_to_all(buffer, ("grp", "dev"), split_axis=0, concat_axis=0, tiled=True)
    partial_rows = half_expert(
        received.reshape(-1, width), gate_up_weight[0], down_weight[0]
    ).reshape(2 * experts, capacity, width)
    returned = lax.all_to_all(partial_rows, ("grp", "dev"), split_axis=0, concat_axis=0, tiled=True)
    flat = returned.reshape(-1, width)
    contract = (((0,), (0,)), ((), ()))
    routed = lax.dot_general(both[0], flat, contract, preferred_element_type=F32) + lax.dot_general(
        both[1], flat, contract, preferred_element_type=F32
    )
    return (attended, routed.astype(BF16))


def solution(mesh):
    row = P(("grp", "dev"), None)
    cube = P(("grp", "dev"), None, None)
    return jax.shard_map(
        on_device,
        mesh=mesh,
        in_specs=(row, row, row, row, P("grp", "dev", None), P("grp", "dev", None), P(), P(), row, row, cube, cube),
        out_specs=(row, row),
        check_vma=False,
    )
```

time: 521 us -> 327 us (0.63); the launches traced: 514 us -> 325 us
  waiting for transfers between devices: 254 us -> 106 us
  local copies, waits for them, and re-layouts: 68.5 us -> 15.6 us
  Pallas kernels: 0 us -> 40.7 us
  other arithmetic: 18 us -> 2.69 us
  between operations: 14.5 us -> 0.71 us
    all_gather x2 -> x0, waiting for transfers between devices: 145 us -> none  [the longest x1 77.1 us: on_device(): lax.all_gather(prefix_keys[0], 'dev', axis=0, tiled=True)]
    pallas_call x0 -> x1, Pallas kernels: none -> 40.7 us  [attention(): pl.pallas_call(attention_kernel, out_shape=(jax.ShapeDtypeStruct((128, 20...]
    scatter x1 -> x0, local copies, waits for them, and re-layouts: 23.5 us -> none  [on_device(): jnp.zeros((experts * capacity, width), jnp.bfloat16).at[slots]]
    all_gather x2 -> x0, local copies, waits for them, and re-layouts: 12.8 us -> none  [the longest x1 6.41 us: on_device(): lax.all_gather(prefix_values[0], 'dev', axis=0, tiled=True)]
    gather x1 -> x0, local copies, waits for them, and re-layouts: 9.82 us -> none  [on_device(): picked = expert_table[slots].astype(jnp.float32)]
    reduce_sum x4 -> x1, other arithmetic: 9.44 us -> 0.9 us  [on_device(): member = jnp.sum(named.astype(F32), axis=0)]
    convert_element_type x1 -> x0, local copies, waits for them, and re-layouts: 6.55 us -> none  [on_device(): picked = expert_table[slots].astype(jnp.float32)]
    dot_general x7 -> x6, matrix products: 45.2 us -> 44.4 us  [the longest x1 17.4 us: half_expert(): projected = jnp.dot(rows, gate_up, preferred_element_type=F32)]
  transfers between devices with their start and end apart: 3 -> 1, of which waited for: 3 -> 1; matrix products, arithmetic and copies ran while one was open for 4% -> 0% of each run, Pallas kernels for 0% -> 0%
where the time goes in v1:
time: 327 us; the launch traced here: 325 us
  blocking collectives  107 us (33%)
  waiting for transfers between devices  106 us (32%)
  matrix products  44.4 us (14%)
  Pallas kernels  40.7 us (12%)
  local copies, waits for them, and re-layouts  15.6 us (5%)
  starting transfers between devices  7.56 us (2%)
    all_to_all x1, blocking collectives, on_device(): lax.all_to_all(buffer, ('grp', 'dev'), split_axis=0, concat_axis=0, tiled...  107 us
    all_to_all x1, waiting for transfers between devices, on_device(): lax.all_to_all(partial_rows, ('grp', 'dev'), split_axis=0, concat_axis=0,...  106 us
    pallas_call x1, Pallas kernels, attention(): pl.pallas_call(attention_kernel, out_shape=(jax.ShapeDtypeStruct((128, 20...  40.7 us
    dot_general x1, matrix products, half_expert(): projected = jnp.dot(rows, gate_up, preferred_element_type=F32)  17.4 us
    dot_general x1, matrix products, half_expert(): return jnp.dot(active, down_proj, preferred_element_type=F32).astype(BF16)  13.5 us
    all_to_all x1, starting transfers between devices, on_device(): lax.all_to_all(partial_rows, ('grp', 'dev'), split_axis=0, concat_axis=0,...  7.56 us
    unnamed x23, local copies, waits for them, and re-layouts  7.48 us
    broadcast_in_dim x1, local copies, waits for them, and re-layouts, on_device(): jnp.broadcast_to(outgoing.reshape(experts, 1, capacity, width), (experts,...  6.87 us
  transfers between devices with their start and end apart: 1, of which 1 were waited for; matrix products, arithmetic and copies ran while one was open for 0% of the time, Pallas kernels for 0%

profile of v1, /device:TPU:1, one launch (start us, length us, event | category | flops | bytes accessed | tf_op | source)
XLA Modules:
  0.0 325.2 jit_solution(4939523722167696219)
XLA Ops:
  0.6 0.9 convert_reduce_fusion
  1.5 0.1 convolution_select_fusion
  1.8 0.2 bitcast_compare_fusion
  2.0 1.0 copy-done.1
  3.0 1.0 copy-done.2
  4.1 1.0 copy-done.3
  5.1 1.0 copy-done.4
  6.2 0.9 copy-done.5
  7.1 0.9 copy-done.6
  8.0 0.7 copy-done.7
  8.7 40.7 %attention.1 = (bf16[128,2048]{1,0:T(8,128)(2,1)S(1)}, bf16[128,2048]{1,0:T(8,128)(2,1)S(1)}) custom-call(bf16[128,2048]{1,0:T(8,128)(2,1)S(1)} %copy-done.1, bf16[32,2048]{1,0:T(8,128)(2,1)S(1)} %bitcast.27, bf16[32,2048]{1,0:T(8,128)(2,1)S(1)} %bitcast.28, bf16[128,2048]{1,0:T(8,128)(2,1)S(1)} %copy-done.2, bf16[128,2048]{1,0:T(8,128)(2,1)S(1)} %copy-done.3, ...), custom_call_target="tpu_custom_call" | custom-call | tf_op jit(solution)/shard_map/attention/pallas_call | solution.py:162
  49.4 3.2 convolution_convert_fusion.1
  52.6 6.9 %broadcast_in_dim.63 = bf16[64,2,16,2048]{3,2,1,0:T(8,128)(2,1)} broadcast(bf16[64,16,2048]{2,1,0:T(8,128)(2,1)} %bitcast.31), dimensions={0,2,3} | broadcast | bytes 12582912 | tf_op jit(solution)/shard_map/broadcast_in_dim | solution.py:224
  59.4 107.4 %all_to_all.10 = bf16[128,16,2048]{2,1,0:T(8,128)(2,1)} all-to-all(bf16[128,16,2048]{2,1,0:T(8,128)(2,1)} %bitcast.30), channel_id=1, replica_groups=mesh['grp'=4,'dev'=32] {'grp','dev'}, dimensions={0} | all-to-all | bytes 16777216 | tf_op jit(solution)/shard_map/all_to_all | solution.py:227
  166.8 17.4 %fusion.1 = f32[2048,1408]{0,1:T(8,128)} fusion(bf16[2048,2048]{1,0:T(8,128)(2,1)} %bitcast.33, bf16[1,2048,1408]{2,1,0:T(8,128)(2,1)S(1)} %bitcast.39), kind=kOutput, calls=%fused_computation.3 | convolution fusion | flops 11811160064 | bytes 25690112 | tf_op jit(solution)/shard_map/dot_general | solution.py:194
  184.2 13.5 %convolution_convert_fusion = bf16[2048,2048]{1,0:T(8,128)(2,1)} fusion(f32[2048,1408]{0,1:T(8,128)} %fusion.1, bf16[1,704,2048]{2,1,0:T(8,128)(2,1)S(1)} %copy-done), kind=kOutput, calls=%fused_computation | convolution fusion | flops 5918425088 | bytes 22806528 | tf_op jit(solution)/shard_map/dot_general | solution.py:196
  197.7 7.6 %all-to-all-start.1 = ((bf16[128,16,2048]{2,1,0:T(8,128)(2,1)}), bf16[128,16,2048]{2,1,0:T(8,128)(2,1)}, u32[]{:S(2)}, u32[]{:S(2)}) async-start(bf16[128,16,2048]{2,1,0:T(8,128)(2,1)} %bitcast.32), calls=%async_computation.1 | async-start | bytes 16777216 | tf_op jit(solution)/shard_map/all_to_all | solution.py:231
  205.3 0.8 select_convert_fusion
  206.1 0.8 fusion.7
  206.9 106.2 %all-to-all-done.1 = bf16[128,16,2048]{2,1,0:T(8,128)(2,1)} async-done(((bf16[128,16,2048]{2,1,0:T(8,128)(2,1)}), bf16[128,16,2048]{2,1,0:T(8,128)(2,1)}, u32[]{:S(2)}, u32[]{:S(2)}) %all-to-all-start.1) | async-done | bytes 8388640 | tf_op jit(solution)/shard_map/all_to_all | solution.py:231
  313.1 1.1 broadcast_in_dim.60
  314.2 4.7 %fusion.10 = f32[128,2048]{1,0:T(8,128)S(1)} fusion(bf16[2048,128]{1,0:T(8,128)(2,1)S(1)} %bitcast.35, bf16[2048,2048]{1,0:T(8,128)(2,1)} %bitcast.13), kind=kOutput, calls=%fused_computation.22 | convolution fusion | flops 1073741824 | bytes 9961472 | tf_op jit(solution)/shard_map/dot_general | solution.py:234
  319.0 5.5 %fusion.6 = bf16[128,2048]{1,0:T(8,128)(2,1)} fusion(f32[128,2048]{1,0:T(8,128)S(1)} %fusion.10, bf16[2048,128]{1,0:T(8,128)(2,1)S(1)} %bitcast.34, bf16[2048,2048]{1,0:T(8,128)(2,1)} %bitcast.13), kind=kOutput, calls=%fused_computation.9 | convolution fusion | flops 1074266112 | bytes 10485760 | tf_op jit(solution)/shard_map/dot_general | solution.py:234
  324.4 0.8 copy.17
  (19 shorter events, 0.2 us)
Async XLA Ops:
  0.6 183.6 %copy-start = (bf16[1,704,2048]{2,1,0:T(8,128)(2,1)S(1)}, bf16[1,704,2048]{2,1,0:T(8,128)(2,1)}, u32[]{:S(2)}) copy-start(bf16[1,704,2048]{2,1,0:T(8,128)(2,1)} %param.23) | copy-start | bytes 8650756
  2.0 1.0 copy-start.1
  3.0 1.0 copy-start.2
  4.1 1.0 copy-start.3
  5.1 1.0 copy-start.4
  6.2 0.9 copy-start.5
  7.1 0.9 copy-start.6
  8.0 0.7 copy-start.7
  52.6 114.3 %slice-start = ((s8[5767168]{0:T(1024)(128)(4,1)}), s8[1572864]{0:T(1024)(128)(4,1)S(1)}, s32[]{:S(2)}) async-start(s8[5767168]{0:T(1024)(128)(4,1)} %bitcast.38), calls=%async_computation.2 | async-start | bytes 3145728
  59.4 107.4 %slice-start.1 = ((s8[5767168]{0:T(1024)(128)(4,1)}), s8[4194304]{0:T(1024)(128)(4,1)S(1)}, s32[]{:S(2)}) async-start(s8[5767168]{0:T(1024)(128)(4,1)} %bitcast.38), calls=%async_computation.3 | async-start | bytes 8388608
  197.7 115.4 %all-to-all-start.1 = ((bf16[128,16,2048]{2,1,0:T(8,128)(2,1)}), bf16[128,16,2048]{2,1,0:T(8,128)(2,1)}, u32[]{:S(2)}, u32[]{:S(2)}) async-start(bf16[128,16,2048]{2,1,0:T(8,128)(2,1)} %bitcast.32), calls=%async_computation.1 | async-start | bytes 16777216 | tf_op jit(solution)/shard_map/all_to_all | solution.py:231
  313.1 5.8 %copy-start.8 = (bf16[64,16,128]{2,1,0:T(8,128)(2,1)S(1)}, bf16[64,16,128]{2,1,0:T(8,128)(2,1)}, u32[]{:S(2)}) copy-start(bf16[64,16,128]{2,1,0:T(8,128)(2,1)} %fusion.7) | copy-start | bytes 786436

commit v2 on v1

--- a/solution.py
+++ b/solution.py
@@ -189,11 +189,15 @@
     )(q, k, v, sk, sv, tok, gain, ow)
 
 
-def half_expert(rows, gate_up, down_proj):
-    hidden_units = down_proj.shape[0]
+def activation(rows, gate_up):
+    hidden_units = gate_up.shape[1] // 2
     projected = jnp.dot(rows, gate_up, preferred_element_type=F32)
-    active = (jax.nn.silu(projected[:, :hidden_units]) * projected[:, hidden_units:]).astype(BF16)
-    return jnp.dot(active, down_proj, preferred_element_type=F32).astype(BF16)
+    return (jax.nn.silu(projected[:, :hidden_units]) * projected[:, hidden_units:]).astype(BF16)
+
+
+AXES = ("grp", "dev")
+SWAP = [(i, i ^ 1) for i in range(128)]
+SERVED = [[i for i in range(128) if i % 4 in xs] for xs in ((0, 3), (1, 2))]
 
 
 def on_device(
@@ -202,38 +206,60 @@
 ):
     rows_here, width = tokens.shape
     experts, capacity = 64, 16
+    own_down = down_weight[0]
+    partner_down = lax.ppermute(own_down, AXES, SWAP)
     named = routes.T[:, None, :] == jnp.arange(experts, dtype=jnp.int32)[None, :, None]
     member = jnp.sum(named.astype(F32), axis=0)
     gate = jnp.sum(jnp.where(named, route_weights.T[:, None, :], 0.0), axis=0)
     before = (jnp.arange(rows_here)[:, None] < jnp.arange(rows_here)[None, :]).astype(BF16)
     rank = jnp.dot(member.astype(BF16), before, preferred_element_type=F32)
     position = jnp.where(member > 0, rank, -1.0)
-    place = position[:, None, :] == jnp.arange(capacity, dtype=F32)[None, :, None]
-    selected = place.astype(BF16).reshape(experts * capacity, rows_here)
-    weights = jnp.where(place, gate[:, None, :], 0.0)
+    slot = jnp.arange(capacity, dtype=F32)
+    twice = jnp.broadcast_to(position[:, None, :], (experts, 2, rows_here))
+    selected = (twice[:, :, None, :] == slot[None, None, :, None]).astype(BF16)
+    selected = selected.reshape(2 * experts * capacity, rows_here)
+    weights = jnp.where(position[:, None, :] == slot[None, :, None], gate[:, None, :], 0.0)
+    weights = weights.reshape(experts * capacity, rows_here)
     high = weights.astype(BF16)
     low = (weights - high.astype(F32)).astype(BF16)
-    both = jnp.stack([high, low])[:, :, None]
-    both = jnp.broadcast_to(both, (2, experts, 2, capacity, rows_here)).reshape(2, 2 * experts * capacity, rows_here)
+    both = jnp.concatenate([high, low], axis=1)
 
     attended, normed = attention(
         queries, prefix_keys[0], prefix_values[0], suffix_keys, suffix_values, tokens,
         norm_gain.reshape(1, width), out_weight,
     )
     outgoing = jnp.dot(selected, normed, preferred_element_type=F32).astype(BF16)
-    buffer = jnp.broadcast_to(
-        outgoing.reshape(experts, 1, capacity, width), (experts, 2, capacity, width)
-    ).reshape(2 * experts, capacity, width)
-    received = lax.all_to_all(buffer, ("grp", "dev"), split_axis=0, concat_axis=0, tiled=True)
-    partial_rows = half_expert(
-        received.reshape(-1, width), gate_up_weight[0], down_weight[0]
-    ).reshape(2 * experts, capacity, width)
-    returned = lax.all_to_all(partial_rows, ("grp", "dev"), split_axis=0, concat_axis=0, tiled=True)
+    received = lax.all_to_all(
+        outgoing.reshape(2 * experts, capacity, width), AXES, split_axis=0, concat_axis=0, tiled=True
+    )
+    by_x = received.reshape(experts // 2, 4, capacity, width)
+    x = lax.axis_index("dev") % 4
+    outer = (x % 3 == 0).astype(jnp.int32)
+    mine = (1 - outer, 2 + outer)
+    others = (outer, 3 - outer)
+
+    def act_of(at):
+        rows = lax.dynamic_index_in_dim(by_x, at, axis=1, keepdims=False)
+        return activation(rows.reshape(-1, width), gate_up_weight[0])
+
+    swapped = []
+    for at in others:
+        swapped.append(lax.ppermute(act_of(at), AXES, SWAP))
+    kept = [act_of(at) for at in mine]
+    finished = [
+        (
+            jnp.dot(k, own_down, preferred_element_type=F32)
+            + jnp.dot(s, partner_down, preferred_element_type=F32)
+        ).astype(BF16).reshape(experts // 2, 1, capacity, width)
+        for k, s in zip(kept, swapped)
+    ]
+    partial_rows = jnp.concatenate(finished, axis=1).reshape(experts, capacity, width)
+    returned = lax.all_to_all(
+        partial_rows, AXES, split_axis=0, concat_axis=0, axis_index_groups=SERVED, tiled=True
+    )
     flat = returned.reshape(-1, width)
-    contract = (((0,), (0,)), ((), ()))
-    routed = lax.dot_general(both[0], flat, contract, preferred_element_type=F32) + lax.dot_general(
-        both[1], flat, contract, preferred_element_type=F32
-    )
+    parts = lax.dot_general(both, flat, (((0,), (0,)), ((), ())), preferred_element_type=F32)
+    routed = parts[:rows_here] + parts[rows_here:]
     return (attended, routed.astype(BF16))
 
 

time: 327 us -> 343 us (1.049)
  blocking collectives: 107 us -> 0 us
  waiting for transfers between devices: 106 us -> 205 us
  starting transfers between devices: 7.56 us -> 24.7 us
  matrix products: 44.4 us -> 50.3 us
    all_to_all x1 -> x0, blocking collectives: 107 us -> none  [on_device(): lax.all_to_all(buffer, ('grp', 'dev'), split_axis=0, concat_axis=0, tiled...]
    all_to_all x1 -> x2, waiting for transfers between devices: 106 us -> 167 us  [the longest x1 106 us: on_device(): lax.all_to_all(outgoing.reshape(2 * experts, capacity, width), AXES, spli...]
    ppermute x0 -> x3, waiting for transfers between devices: none -> 38 us  [the longest x2 27 us: on_device(): swapped.append(lax.ppermute(act_of(at), AXES, SWAP))]
    all_to_all x1 -> x2, starting transfers between devices: 7.56 us -> 21.3 us  [the longest x1 12.5 us: on_device(): lax.all_to_all(partial_rows, AXES, split_axis=0, concat_axis=0, axis_inde...]
    broadcast_in_dim x3 -> x0, local copies, waits for them, and re-layouts: 8 us -> none  [the longest x1 6.87 us: on_device(): jnp.broadcast_to(outgoing.reshape(experts, 1, capacity, width), (experts,...]
    dynamic_slice x0 -> x1, local copies, waits for them, and re-layouts: none -> 6.03 us  [act_of(): rows = lax.dynamic_index_in_dim(by_x, at, axis=1, keepdims=False)]
    dot_general x4 -> x9, matrix products: 41.1 us -> 44.6 us  [the longest x4 23.3 us: activation(): projected = jnp.dot(rows, gate_up, preferred_element_type=F32)]
    unnamed x23 -> x21, local copies, waits for them, and re-layouts: 7.48 us -> 7.47 us
  transfers between devices with their start and end apart: 1 -> 5, of which waited for: 1 -> 5; matrix products, arithmetic and copies ran while one was open for 0% -> 14% of each run, Pallas kernels for 0% -> 0%
where the time goes in v2:
time: 343 us; the launch traced here: 342 us
  waiting for transfers between devices  205 us (60%)
  matrix products  50.3 us (15%)
  Pallas kernels  40.7 us (12%)
  starting transfers between devices  24.7 us (7%)
  local copies, waits for them, and re-layouts  15.1 us (4%)
  other arithmetic  5.74 us (2%)
    all_to_all x1, waiting for transfers between devices, on_device(): lax.all_to_all(outgoing.reshape(2 * experts, capacity, width), AXES, spli...  106 us
    all_to_all x1, waiting for transfers between devices, on_device(): lax.all_to_all(partial_rows, AXES, split_axis=0, concat_axis=0, axis_inde...  60.5 us
    pallas_call x1, Pallas kernels, attention(): pl.pallas_call(attention_kernel, out_shape=(jax.ShapeDtypeStruct((128, 20...  40.7 us
    ppermute x2, waiting for transfers between devices, on_device(): swapped.append(lax.ppermute(act_of(at), AXES, SWAP))  27 us
    dot_general x4, matrix products, activation(): projected = jnp.dot(rows, gate_up, preferred_element_type=F32)  23.3 us
    all_to_all x1, starting transfers between devices, on_device(): lax.all_to_all(partial_rows, AXES, split_axis=0, concat_axis=0, axis_inde...  12.5 us
    ppermute x1, waiting for transfers between devices, on_device(): partner_down = lax.ppermute(own_down, AXES, SWAP)  11 us
    dot_general x2, matrix products, on_device(): jnp.dot(k, own_down, preferred_element_type=F32)  10.3 us
  transfers between devices with their start and end apart: 5, of which 5 were waited for; matrix products, arithmetic and copies ran while one was open for 14% of the time, Pallas kernels for 0%

profile of v2, /device:TPU:1, one launch (start us, length us, event | category | flops | bytes accessed | tf_op | source)
XLA Modules:
  0.0 341.9 jit_solution(13613539063261316039)
XLA Ops:
  3.1 1.0 copy-done.1
  8.7 40.7 %attention.1 = (bf16[128,2048]{1,0:T(8,128)(2,1)S(1)}, bf16[128,2048]{1,0:T(8,128)(2,1)S(1)}) custom-call(bf16[128,2048]{1,0:T(8,128)(2,1)S(1)} %copy-done, bf16[32,2048]{1,0:T(8,128)(2,1)S(1)} %bitcast.64, bf16[32,2048]{1,0:T(8,128)(2,1)S(1)} %bitcast.65, bf16[128,2048]{1,0:T(8,128)(2,1)S(1)} %copy-done.1, bf16[128,2048]{1,0:T(8,128)(2,1)S(1)} %copy-done.2, ...), custom_call_target="tpu_custom_call" | custom-call | tf_op jit(solution)/shard_map/attention/pallas_call | solution.py:162
  49.4 5.6 %convolution_convert_fusion = bf16[2048,2048]{1,0:T(8,128)(2,1)} fusion(pred[2048,128]{1,0:T(32,128)(4,1)S(1)} %bitcast_compare_fusion, bf16[128,2048]{1,0:T(8,128)(2,1)S(1)} %get-tuple-element.5), kind=kOutput, calls=%fused_computation | convolution fusion | flops 1077936128 | bytes 9175040 | tf_op jit(solution)/shard_map/dot_general | solution.py:231
  54.9 8.8 %all-to-all-start = ((bf16[128,16,2048]{2,1,0:T(8,128)(2,1)}), bf16[128,16,2048]{2,1,0:T(8,128)(2,1)}, u32[]{:S(2)}, u32[]{:S(2)}) async-start(bf16[128,16,2048]{2,1,0:T(8,128)(2,1)} %bitcast.67), calls=%async_computation | async-start | bytes 16777216 | tf_op jit(solution)/shard_map/all_to_all | solution.py:232
  63.8 1.6 collective-permute-start.1
  65.4 106.1 %all-to-all-done = bf16[128,16,2048]{2,1,0:T(8,128)(2,1)} async-done(((bf16[128,16,2048]{2,1,0:T(8,128)(2,1)}), bf16[128,16,2048]{2,1,0:T(8,128)(2,1)}, u32[]{:S(2)}, u32[]{:S(2)}) %all-to-all-start) | async-done | bytes 8388640 | tf_op jit(solution)/shard_map/all_to_all | solution.py:232
  171.5 6.0 %constant_dynamic-slice_fusion.2 = (bf16[32,1,16,2048]{3,2,1,0:T(8,128)(2,1)S(1)}, bf16[32,1,16,2048]{3,2,1,0:T(8,128)(2,1)S(1)}, bf16[32,1,16,2048]{3,2,1,0:T(8,128)(2,1)S(1)}, bf16[32,1,16,2048]{3,2,1,0:T(8,128)(2,1)}) fusion(bf16[32,4,16,2048]{3,2,1,0:T(8,128)(2,1)} %bitcast.9, s32[]{:T(128)S(6)} %select_n.43, s32[]{:T(128)S(6)} %select_n.45, ...), kind=kLoop, calls=%fused_computation.44 | loop fusion | bytes 16777232 | tf_op jit(solution)/shard_map/jit(dynamic_index_in_dim)/dynamic_slice | solution.py:242
  177.6 5.9 %fusion.2 = f32[512,1408]{1,0:T(8,128)S(1)} fusion(bf16[512,2048]{1,0:T(8,128)(2,1)S(1)} %bitcast.72, bf16[1,2048,1408]{2,1,0:T(8,128)(2,1)} %param.22), kind=kOutput, calls=%fused_computation.3 | convolution fusion | flops 2952790016 | bytes 10747904 | tf_op jit(solution)/shard_map/dot_general | solution.py:194
  183.4 5.7 %fusion.15 = f32[512,2048]{1,0:T(8,128)} fusion(f32[512,1408]{1,0:T(8,128)S(1)} %fusion.2, bf16[1,704,2048]{2,1,0:T(8,128)(2,1)} %param.23), kind=kOutput, calls=%fused_computation.25 | convolution fusion | flops 1478557696 | bytes 10223616 | tf_op jit(solution)/shard_map/dot_general | solution.py:251
  189.1 3.4 fusion
  193.0 1.1 copy.21
  194.2 8.3 %fusion.6 = f32[512,1408]{1,0:T(8,128)} fusion(bf16[512,2048]{1,0:T(8,128)(2,1)} %bitcast.70, bf16[1,2048,1408]{2,1,0:T(8,128)(2,1)} %param.22), kind=kOutput, calls=%fused_computation.7 | convolution fusion | flops 2952790016 | bytes 10747904 | tf_op jit(solution)/shard_map/dot_general | solution.py:194
  202.4 5.7 %fusion.4 = f32[512,1408]{1,0:T(8,128)S(1)} fusion(bf16[512,2048]{1,0:T(8,128)(2,1)S(1)} %bitcast.69, bf16[1,2048,1408]{2,1,0:T(8,128)(2,1)} %param.22), kind=kOutput, calls=%fused_computation.5 | convolution fusion | flops 2952790016 | bytes 10747904 | tf_op jit(solution)/shard_map/dot_general | solution.py:194
  208.9 1.8 collective-permute-start
  210.7 4.6 %fusion.13 = f32[512,2048]{1,0:T(8,128)S(1)} fusion(f32[512,1408]{1,0:T(8,128)} %fusion.6, bf16[1,704,2048]{2,1,0:T(8,128)(2,1)} %param.23), kind=kOutput, calls=%fused_computation.24 | convolution fusion | flops 1478557696 | bytes 10223616 | tf_op jit(solution)/shard_map/dot_general | solution.py:251
  215.3 11.0 %collective-permute-done.1 = bf16[704,2048]{1,0:T(8,128)(2,1)} collective-permute-done((bf16[704,2048]{1,0:T(8,128)(2,1)}, bf16[704,2048]{1,0:T(8,128)(2,1)}, u32[]{:S(2)}, u32[]{:S(2)}) %collective-permute-start.1) | collective-permute-done | bytes 2883616 | tf_op jit(solution)/shard_map/ppermute | solution.py:210
  226.3 15.3 %collective-permute-done.2 = bf16[512,704]{0,1:T(8,128)(2,1)S(1)} collective-permute-done((bf16[512,704]{0,1:T(8,128)(2,1)}, bf16[512,704]{0,1:T(8,128)(2,1)S(1)}, u32[]{:S(2)}, u32[]{:S(2)}) %collective-permute-start.2) | collective-permute-done | bytes 720928 | tf_op jit(solution)/shard_map/ppermute | solution.py:247
  241.7 3.8 %add_convert_fusion = bf16[512,2048]{1,0:T(8,128)(2,1)S(1)} fusion(f32[512,2048]{1,0:T(8,128)S(1)} %copy-done.7, bf16[512,704]{0,1:T(8,128)(2,1)S(1)} %collective-permute-done.2, bf16[704,2048]{1,0:T(8,128)(2,1)} %collective-permute-done.1), kind=kOutput, calls=%fused_computation.10 | convolution fusion | flops 1478492160 | bytes 9895936 | tf_op jit(solution)/shard_map/dot_general | solution.py:252
  245.5 11.7 %collective-permute-done = bf16[512,704]{0,1:T(8,128)(2,1)S(1)} collective-permute-done((bf16[512,704]{0,1:T(8,128)(2,1)S(1)}, bf16[512,704]{0,1:T(8,128)(2,1)S(1)}, u32[]{:S(2)}, u32[]{:S(2)}) %collective-permute-start) | collective-permute-done | bytes 720928 | tf_op jit(solution)/shard_map/ppermute | solution.py:247
  257.1 3.8 %add_convert_fusion.1 = bf16[512,2048]{1,0:T(8,128)(2,1)S(1)} fusion(f32[512,2048]{1,0:T(8,128)S(1)} %fusion.13, bf16[512,704]{0,1:T(8,128)(2,1)S(1)} %collective-permute-done, bf16[704,2048]{1,0:T(8,128)(2,1)} %collective-permute-done.1), kind=kOutput, calls=%fused_computation.11 | convolution fusion | flops 1478492160 | bytes 9895936 | tf_op jit(solution)/shard_map/dot_general | solution.py:252
  260.9 2.3 pad_maximum_fusion
  263.3 12.5 %all-to-all-start.1 = ((bf16[64,16,2048]{2,1,0:T(8,128)(2,1)}), bf16[64,16,2048]{2,1,0:T(8,128)(2,1)}, u32[]{:S(2)}, u32[]{:S(2)}) async-start(bf16[64,16,2048]{2,1,0:T(8,128)(2,1)} %bitcast.68), calls=%async_computation.1 | async-start | bytes 8388608 | tf_op jit(solution)/shard_map/all_to_all | solution.py:257
  276.3 60.5 %all-to-all-done.1 = bf16[64,16,2048]{2,1,0:T(8,128)(2,1)} async-done(((bf16[64,16,2048]{2,1,0:T(8,128)(2,1)}), bf16[64,16,2048]{2,1,0:T(8,128)(2,1)}, u32[]{:S(2)}, u32[]{:S(2)}) %all-to-all-start.1) | async-done | bytes 4194336 | tf_op jit(solution)/shard_map/all_to_all | solution.py:257
  336.7 3.5 %fusion.19 = f32[256,2048]{1,0:T(8,128)S(1)} fusion(bf16[1024,2048]{1,0:T(8,128)(2,1)} %bitcast.21, bf16[1024,128]{1,0:T(8,128)(2,1)S(1)} %fusion.25, bf16[1024,128]{1,0:T(8,128)(2,1)S(1)} %fusion.24), kind=kOutput, calls=%fused_computation.28 | convolution fusion | flops 1074790400 | bytes 6815744 | tf_op jit(solution)/shard_map/dot_general | solution.py:261
  (35 shorter events, 10.5 us)
Async XLA Ops:
  2.0 1.0 copy-start
  3.1 1.0 copy-start.1
  4.1 1.0 copy-start.2
  5.2 1.0 copy-start.3
  6.2 0.9 copy-start.4
  7.1 0.9 copy-start.5
  8.0 0.7 copy-start.6
  54.9 116.6 %all-to-all-start = ((bf16[128,16,2048]{2,1,0:T(8,128)(2,1)}), bf16[128,16,2048]{2,1,0:T(8,128)(2,1)}, u32[]{:S(2)}, u32[]{:S(2)}) async-start(bf16[128,16,2048]{2,1,0:T(8,128)(2,1)} %bitcast.67), calls=%async_computation | async-start | bytes 16777216 | tf_op jit(solution)/shard_map/all_to_all | solution.py:232
  63.8 162.6 %collective-permute-start.1 = (bf16[704,2048]{1,0:T(8,128)(2,1)}, bf16[704,2048]{1,0:T(8,128)(2,1)}, u32[]{:S(2)}, u32[]{:S(2)}) collective-permute-start(bf16[704,2048]{1,0:T(8,128)(2,1)} %bitcast.12), channel_id=1, source_target_pairs={{0,1},{1,0},{2,3},{3,2},{4,5},{5,4},{6,7},{7,6},{8,9},{9,8},{10,11... | collective-permute-start | bytes 8650760 | tf_op jit(solution)/shard_map/ppermute | solution.py:210
  171.5 17.6 %slice-start = ((s8[5767168]{0:T(1024)(128)(4,1)}), s8[4194304]{0:T(1024)(128)(4,1)S(1)}, s32[]{:S(2)}) async-start(s8[5767168]{0:T(1024)(128)(4,1)} %bitcast.77), calls=%async_computation.2 | async-start | bytes 8388608
  177.6 11.6 %slice-start.1 = ((s8[5767168]{0:T(1024)(128)(4,1)}), s8[1572864]{0:T(1024)(128)(4,1)S(1)}, s32[]{:S(2)}) async-start(s8[5767168]{0:T(1024)(128)(4,1)} %bitcast.77), calls=%async_computation.3 | async-start | bytes 3145728
  194.2 47.5 %collective-permute-start.2 = (bf16[512,704]{0,1:T(8,128)(2,1)}, bf16[512,704]{0,1:T(8,128)(2,1)S(1)}, u32[]{:S(2)}, u32[]{:S(2)}) collective-permute-start(bf16[512,704]{0,1:T(8,128)(2,1)} %copy.21), channel_id=1, source_target_pairs={{0,1},{1,0},{2,3},{3,2},{4,5},{5,4},{6,7},{7,6},{8,9},{9,8},{10,11... | collective-permute-start | bytes 2162696 | tf_op jit(solution)/shard_map/ppermute | solution.py:247
  208.9 32.7 %copy-start.7 = (f32[512,2048]{1,0:T(8,128)S(1)}, f32[512,2048]{1,0:T(8,128)}, u32[]{:S(2)}) copy-start(f32[512,2048]{1,0:T(8,128)} %fusion.15) | copy-start | bytes 12582916
  208.9 48.2 %collective-permute-start = (bf16[512,704]{0,1:T(8,128)(2,1)S(1)}, bf16[512,704]{0,1:T(8,128)(2,1)S(1)}, u32[]{:S(2)}, u32[]{:S(2)}) collective-permute-start(bf16[512,704]{0,1:T(8,128)(2,1)S(1)} %copy.20), channel_id=1, source_target_pairs={{0,1},{1,0},{2,3},{3,2},{4,5},{5,4},{6,7},{7,6},{8,9},{9,8},{10,11... | collective-permute-start | bytes 2162696 | tf_op jit(solution)/shard_map/ppermute | solution.py:247
  263.3 73.4 %all-to-all-start.1 = ((bf16[64,16,2048]{2,1,0:T(8,128)(2,1)}), bf16[64,16,2048]{2,1,0:T(8,128)(2,1)}, u32[]{:S(2)}, u32[]{:S(2)}) async-start(bf16[64,16,2048]{2,1,0:T(8,128)(2,1)} %bitcast.68), calls=%async_computation.1 | async-start | bytes 8388608 | tf_op jit(solution)/shard_map/all_to_all | solution.py:257

commit v3 on v1

--- a/solution.py
+++ b/solution.py
@@ -196,45 +196,54 @@
     return jnp.dot(active, down_proj, preferred_element_type=F32).astype(BF16)
 
 
+AXES = ("grp", "dev")
+CHUNKS = 2
+
+
 def on_device(
     tokens, queries, suffix_keys, suffix_values, prefix_keys, prefix_values,
     out_weight, norm_gain, routes, route_weights, gate_up_weight, down_weight,
 ):
     rows_here, width = tokens.shape
     experts, capacity = 64, 16
+    depth = capacity // CHUNKS
     named = routes.T[:, None, :] == jnp.arange(experts, dtype=jnp.int32)[None, :, None]
     member = jnp.sum(named.astype(F32), axis=0)
     gate = jnp.sum(jnp.where(named, route_weights.T[:, None, :], 0.0), axis=0)
     before = (jnp.arange(rows_here)[:, None] < jnp.arange(rows_here)[None, :]).astype(BF16)
     rank = jnp.dot(member.astype(BF16), before, preferred_element_type=F32)
     position = jnp.where(member > 0, rank, -1.0)
-    place = position[:, None, :] == jnp.arange(capacity, dtype=F32)[None, :, None]
-    selected = place.astype(BF16).reshape(experts * capacity, rows_here)
-    weights = jnp.where(place, gate[:, None, :], 0.0)
-    high = weights.astype(BF16)
-    low = (weights - high.astype(F32)).astype(BF16)
-    both = jnp.stack([high, low])[:, :, None]
-    both = jnp.broadcast_to(both, (2, experts, 2, capacity, rows_here)).reshape(2, 2 * experts * capacity, rows_here)
+
+    def both_halves(a):
+        shape = (experts, 2, depth, rows_here)
+        return jnp.broadcast_to(a.reshape(experts, 1, 1, rows_here), shape)
 
     attended, normed = attention(
         queries, prefix_keys[0], prefix_values[0], suffix_keys, suffix_values, tokens,
         norm_gain.reshape(1, width), out_weight,
     )
-    outgoing = jnp.dot(selected, normed, preferred_element_type=F32).astype(BF16)
-    buffer = jnp.broadcast_to(
-        outgoing.reshape(experts, 1, capacity, width), (experts, 2, capacity, width)
-    ).reshape(2 * experts, capacity, width)
-    received = lax.all_to_all(buffer, ("grp", "dev"), split_axis=0, concat_axis=0, tiled=True)
-    partial_rows = half_expert(
-        received.reshape(-1, width), gate_up_weight[0], down_weight[0]
-    ).reshape(2 * experts, capacity, width)
-    returned = lax.all_to_all(partial_rows, ("grp", "dev"), split_axis=0, concat_axis=0, tiled=True)
-    flat = returned.reshape(-1, width)
-    contract = (((0,), (0,)), ((), ()))
-    routed = lax.dot_general(both[0], flat, contract, preferred_element_type=F32) + lax.dot_general(
-        both[1], flat, contract, preferred_element_type=F32
-    )
-    return (attended, routed.astype(BF16))
+
+    def exchange(rows):
+        return lax.all_to_all(
+            rows.reshape(2 * experts, depth, width), AXES, split_axis=0, concat_axis=0, tiled=True
+        ).reshape(2 * experts * depth, width)
+
+    places, received = [], []
+    for n in range(CHUNKS):
+        slot = jnp.arange(n * depth, (n + 1) * depth, dtype=F32)[None, None, :, None]
+        place = both_halves(position) == slot
+        places.append(place)
+        selected = place.astype(BF16).reshape(2 * experts * depth, rows_here)
+        received.append(exchange(jnp.dot(selected, normed, preferred_element_type=F32).astype(BF16)))
+    returned = [exchange(half_expert(rows, gate_up_weight[0], down_weight[0])) for rows in received]
+    total = jnp.zeros((2 * rows_here, width), F32)
+    for place, rows in zip(places, returned):
+        weights = jnp.where(place, both_halves(gate), 0.0).reshape(2 * experts * depth, rows_here)
+        high = weights.astype(BF16)
+        low = (weights - high.astype(F32)).astype(BF16)
+        both = jnp.concatenate([high, low], axis=1)
+        total = total + lax.dot_general(both, rows, (((0,), (0,)), ((), ())), preferred_element_type=F32)
+    return (attended, (total[:rows_here] + total[rows_here:]).astype(BF16))
 
 
 def solution(mesh):

time: 327 us -> 298 us (0.911)
  blocking collectives: 107 us -> 0 us
  waiting for transfers between devices: 106 us -> 171 us
  starting transfers between devices: 7.56 us -> 26 us
  local copies, waits for them, and re-layouts: 15.6 us -> 8.57 us
    all_to_all x1 -> x0, blocking collectives: 107 us -> none  [on_device(): lax.all_to_all(buffer, ('grp', 'dev'), split_axis=0, concat_axis=0, tiled...]
    all_to_all x1 -> x4, waiting for transfers between devices: 106 us -> 171 us  [exchange(): lax.all_to_all(rows.reshape(2 * experts, depth, width), AXES, split_axis=...]
    all_to_all x1 -> x4, starting transfers between devices: 7.56 us -> 26 us  [exchange(): lax.all_to_all(rows.reshape(2 * experts, depth, width), AXES, split_axis=...]
    broadcast_in_dim x3 -> x0, local copies, waits for them, and re-layouts: 8 us -> none  [the longest x1 6.87 us: on_device(): jnp.broadcast_to(outgoing.reshape(experts, 1, capacity, width), (experts,...]
    dot_general x1 -> x2, matrix products: 17.4 us -> 20.9 us  [half_expert(): projected = jnp.dot(rows, gate_up, preferred_element_type=F32)]
    dot_general x1 -> x2, matrix products: 13.5 us -> 10.4 us  [half_expert(): return jnp.dot(active, down_proj, preferred_element_type=F32).astype(BF16)]
    unnamed x23 -> x27, local copies, waits for them, and re-layouts: 7.48 us -> 8.27 us
  transfers between devices with their start and end apart: 1 -> 4, of which waited for: 1 -> 4; matrix products, arithmetic and copies ran while one was open for 0% -> 13% of each run, Pallas kernels for 0% -> 0%
where the time goes in v3:
time: 298 us; the launch traced here: 297 us
  waiting for transfers between devices  171 us (57%)
  matrix products  46.9 us (16%)
  Pallas kernels  40.7 us (14%)
  starting transfers between devices  26 us (9%)
  local copies, waits for them, and re-layouts  8.57 us (3%)
  other arithmetic  3.47 us (1%)
    all_to_all x4, waiting for transfers between devices, exchange(): lax.all_to_all(rows.reshape(2 * experts, depth, width), AXES, split_axis=...  171 us
    pallas_call x1, Pallas kernels, attention(): pl.pallas_call(attention_kernel, out_shape=(jax.ShapeDtypeStruct((128, 20...  40.7 us
    all_to_all x4, starting transfers between devices, exchange(): lax.all_to_all(rows.reshape(2 * experts, depth, width), AXES, split_axis=...  26 us
    dot_general x2, matrix products, half_expert(): projected = jnp.dot(rows, gate_up, preferred_element_type=F32)  20.9 us
    dot_general x2, matrix products, half_expert(): return jnp.dot(active, down_proj, preferred_element_type=F32).astype(BF16)  10.4 us
    dot_general x2, matrix products, on_device(): lax.dot_general(both, rows, (((0,), (0,)), ((), ())), preferred_element_t...  8.99 us
    unnamed x27, local copies, waits for them, and re-layouts  8.27 us
    dot_general x2, matrix products, on_device(): jnp.dot(selected, normed, preferred_element_type=F32).astype(BF16)  6.41 us
  transfers between devices with their start and end apart: 4, of which 4 were waited for; matrix products, arithmetic and copies ran while one was open for 13% of the time, Pallas kernels for 0%

profile of v3, /device:TPU:1, one launch (start us, length us, event | category | flops | bytes accessed | tf_op | source)
XLA Modules:
  0.0 297.3 jit_solution(17116853662236773005)
XLA Ops:
  1.0 1.5 select_reduce_fusion
  3.0 1.0 copy-done.1
  4.1 1.0 copy-done.2
  5.1 1.0 copy-done.3
  6.1 1.0 copy-done.4
  7.2 0.9 copy-done.7
  9.7 40.7 %attention.1 = (bf16[128,2048]{1,0:T(8,128)(2,1)S(1)}, bf16[128,2048]{1,0:T(8,128)(2,1)S(1)}) custom-call(bf16[128,2048]{1,0:T(8,128)(2,1)S(1)} %copy-done.1, bf16[32,2048]{1,0:T(8,128)(2,1)S(1)} %bitcast.75, bf16[32,2048]{1,0:T(8,128)(2,1)S(1)} %bitcast.76, bf16[128,2048]{1,0:T(8,128)(2,1)S(1)} %copy-done.2, bf16[128,2048]{1,0:T(8,128)(2,1)S(1)} %copy-done.3, ...), custom_call_target="tpu_custom_call" | custom-call | tf_op jit(solution)/shard_map/attention/pallas_call | solution.py:162
  51.2 3.2 %convert_bitcast_fusion.1 = bf16[128,8,2048]{2,1,0:T(8,128)(2,1)} fusion(pred[1024,128]{1,0:T(32,128)(4,1)S(1)} %get-tuple-element.13, bf16[128,2048]{1,0:T(8,128)(2,1)S(1)} %get-tuple-element.5), kind=kOutput, calls=%fused_computation.11 | convolution fusion | flops 538968064 | bytes 4849664 | tf_op jit(solution)/shard_map/dot_general | solution.py:237
  54.4 8.8 %all-to-all-start.2 = ((bf16[128,8,2048]{2,1,0:T(8,128)(2,1)}), bf16[128,8,2048]{2,1,0:T(8,128)(2,1)}, u32[]{:S(2)}, u32[]{:S(2)}) async-start(bf16[128,8,2048]{2,1,0:T(8,128)(2,1)} %convert_bitcast_fusion.1), calls=%async_computation.2 | async-start | bytes 8388608 | tf_op jit(solution)/shard_map/all_to_all | solution.py:227
  63.2 3.2 %convert_bitcast_fusion.3 = bf16[128,8,2048]{2,1,0:T(8,128)(2,1)} fusion(pred[1024,128]{1,0:T(32,128)(4,1)S(1)} %get-tuple-element.12, bf16[128,2048]{1,0:T(8,128)(2,1)S(1)} %get-tuple-element.5), kind=kOutput, calls=%fused_computation.13 | convolution fusion | flops 538968064 | bytes 4849664 | tf_op jit(solution)/shard_map/dot_general | solution.py:237
  66.4 49.5 %all-to-all-done.2 = bf16[128,8,2048]{2,1,0:T(8,128)(2,1)} async-done(((bf16[128,8,2048]{2,1,0:T(8,128)(2,1)}), bf16[128,8,2048]{2,1,0:T(8,128)(2,1)}, u32[]{:S(2)}, u32[]{:S(2)}) %all-to-all-start.2) | async-done | bytes 4194336 | tf_op jit(solution)/shard_map/all_to_all | solution.py:227
  115.9 5.7 %all-to-all-start = ((bf16[128,8,2048]{2,1,0:T(8,128)(2,1)}), bf16[128,8,2048]{2,1,0:T(8,128)(2,1)}, u32[]{:S(2)}, u32[]{:S(2)}) async-start(bf16[128,8,2048]{2,1,0:T(8,128)(2,1)} %convert_bitcast_fusion.3), calls=%async_computation | async-start | bytes 8388608 | tf_op jit(solution)/shard_map/all_to_all | solution.py:227
  121.6 10.4 %fusion = f32[1024,1408]{1,0:T(8,128)S(1)} fusion(bf16[1,2048,1408]{2,1,0:T(8,128)(2,1)} %param.22, bf16[128,8,2048]{2,1,0:T(8,128)(2,1)} %all-to-all-done.2), kind=kOutput, calls=%fused_computation | convolution fusion | flops 5905580032 | bytes 15728640 | tf_op jit(solution)/shard_map/dot_general | solution.py:194
  132.1 5.2 %convert_bitcast_fusion = bf16[128,8,2048]{2,1,0:T(8,128)(2,1)} fusion(bf16[1,704,2048]{2,1,0:T(8,128)(2,1)S(1)} %copy-done, f32[1024,1408]{1,0:T(8,128)S(1)} %fusion), kind=kOutput, calls=%fused_computation.10 | convolution fusion | flops 2959212544 | bytes 13369344 | tf_op jit(solution)/shard_map/dot_general | solution.py:196
  137.3 37.1 %all-to-all-done = bf16[128,8,2048]{2,1,0:T(8,128)(2,1)} async-done(((bf16[128,8,2048]{2,1,0:T(8,128)(2,1)}), bf16[128,8,2048]{2,1,0:T(8,128)(2,1)}, u32[]{:S(2)}, u32[]{:S(2)}) %all-to-all-start) | async-done | bytes 4194336 | tf_op jit(solution)/shard_map/all_to_all | solution.py:227
  174.4 5.7 %all-to-all-start.3 = ((bf16[128,8,2048]{2,1,0:T(8,128)(2,1)}), bf16[128,8,2048]{2,1,0:T(8,128)(2,1)}, u32[]{:S(2)}, u32[]{:S(2)}) async-start(bf16[128,8,2048]{2,1,0:T(8,128)(2,1)} %convert_bitcast_fusion), calls=%async_computation.3 | async-start | bytes 8388608 | tf_op jit(solution)/shard_map/all_to_all | solution.py:227
  180.1 10.4 %fusion.2 = f32[1024,1408]{1,0:T(8,128)S(1)} fusion(bf16[1,2048,1408]{2,1,0:T(8,128)(2,1)} %param.22, bf16[128,8,2048]{2,1,0:T(8,128)(2,1)} %all-to-all-done), kind=kOutput, calls=%fused_computation.2 | convolution fusion | flops 5905580032 | bytes 15728640 | tf_op jit(solution)/shard_map/dot_general | solution.py:194
  190.6 5.2 %convert_bitcast_fusion.2 = bf16[128,8,2048]{2,1,0:T(8,128)(2,1)} fusion(bf16[1,704,2048]{2,1,0:T(8,128)(2,1)S(1)} %copy-done, f32[1024,1408]{1,0:T(8,128)S(1)} %fusion.2), kind=kOutput, calls=%fused_computation.12 | convolution fusion | flops 2959212544 | bytes 13369344 | tf_op jit(solution)/shard_map/dot_general | solution.py:196
  195.8 37.1 %all-to-all-done.3 = bf16[128,8,2048]{2,1,0:T(8,128)(2,1)} async-done(((bf16[128,8,2048]{2,1,0:T(8,128)(2,1)}), bf16[128,8,2048]{2,1,0:T(8,128)(2,1)}, u32[]{:S(2)}, u32[]{:S(2)}) %all-to-all-start.3) | async-done | bytes 4194336 | tf_op jit(solution)/shard_map/all_to_all | solution.py:227
  232.9 5.7 %all-to-all-start.1 = ((bf16[128,8,2048]{2,1,0:T(8,128)(2,1)}), bf16[128,8,2048]{2,1,0:T(8,128)(2,1)}, u32[]{:S(2)}, u32[]{:S(2)}) async-start(bf16[128,8,2048]{2,1,0:T(8,128)(2,1)} %convert_bitcast_fusion.2), calls=%async_computation.1 | async-start | bytes 8388608 | tf_op jit(solution)/shard_map/all_to_all | solution.py:227
  239.4 4.8 %fusion.4 = f32[256,2048]{1,0:T(8,128)} fusion(bf16[128,8,2048]{2,1,0:T(8,128)(2,1)} %all-to-all-done.3, bf16[1024,128]{1,0:T(8,128)(2,1)S(1)} %get-tuple-element.11, bf16[1024,128]{1,0:T(8,128)(2,1)S(1)} %get-tuple-element.9), kind=kOutput, calls=%fused_computation.4 | convolution fusion | flops 1074790400 | bytes 6815744 | tf_op jit(solution)/shard_map/dot_general | solution.py:245
  244.2 47.3 %all-to-all-done.1 = bf16[128,8,2048]{2,1,0:T(8,128)(2,1)} async-done(((bf16[128,8,2048]{2,1,0:T(8,128)(2,1)}), bf16[128,8,2048]{2,1,0:T(8,128)(2,1)}, u32[]{:S(2)}, u32[]{:S(2)}) %all-to-all-start.1) | async-done | bytes 4194336 | tf_op jit(solution)/shard_map/all_to_all | solution.py:227
  291.5 4.2 %fusion.14 = f32[256,2048]{1,0:T(8,128)S(1)} fusion(f32[256,2048]{1,0:T(8,128)} %fusion.4, bf16[128,8,2048]{2,1,0:T(8,128)(2,1)} %all-to-all-done.1, bf16[1024,128]{1,0:T(8,128)(2,1)S(1)} %get-tuple-element.10, bf16[1024,128]{1,0:T(8,128)(2,1)S(1)} %get-tuple-element.8), kind=kOutput, calls=%fused_computation.20 | convolution fusion | flops 1075314688 | bytes 8912896 | tf_op jit(solution)/shard_map/dot_general | solution.py:245
  295.6 0.9 fusion.21
  (31 shorter events, 4.7 us)
Async XLA Ops:
  0.6 131.4 %copy-start = (bf16[1,704,2048]{2,1,0:T(8,128)(2,1)S(1)}, bf16[1,704,2048]{2,1,0:T(8,128)(2,1)}, u32[]{:S(2)}) copy-start(bf16[1,704,2048]{2,1,0:T(8,128)(2,1)} %param.23) | copy-start | bytes 8650756
  2.7 47.7 %copy-start.10 = (f32[64,128]{1,0:T(8,128)}, f32[64,128]{1,0:T(8,128)S(1)}, u32[]{:S(2)}) copy-start(f32[64,128]{1,0:T(8,128)S(1)} %convolution_select_fusion) | copy-start | bytes 98308
  3.0 1.0 copy-start.1
  4.1 1.0 copy-start.2
  5.1 1.0 copy-start.3
  6.1 1.0 copy-start.4
  7.2 0.9 copy-start.7
  8.1 0.9 copy-start.8
  9.0 0.7 copy-start.9
  50.4 0.8 copy-start.5
  54.4 61.5 %all-to-all-start.2 = ((bf16[128,8,2048]{2,1,0:T(8,128)(2,1)}), bf16[128,8,2048]{2,1,0:T(8,128)(2,1)}, u32[]{:S(2)}, u32[]{:S(2)}) async-start(bf16[128,8,2048]{2,1,0:T(8,128)(2,1)} %convert_bitcast_fusion.1), calls=%async_computation.2 | async-start | bytes 8388608 | tf_op jit(solution)/shard_map/all_to_all | solution.py:227
  115.9 58.5 %all-to-all-start = ((bf16[128,8,2048]{2,1,0:T(8,128)(2,1)}), bf16[128,8,2048]{2,1,0:T(8,128)(2,1)}, u32[]{:S(2)}, u32[]{:S(2)}) async-start(bf16[128,8,2048]{2,1,0:T(8,128)(2,1)} %convert_bitcast_fusion.3), calls=%async_computation | async-start | bytes 8388608 | tf_op jit(solution)/shard_map/all_to_all | solution.py:227
  174.4 58.5 %all-to-all-start.3 = ((bf16[128,8,2048]{2,1,0:T(8,128)(2,1)}), bf16[128,8,2048]{2,1,0:T(8,128)(2,1)}, u32[]{:S(2)}, u32[]{:S(2)}) async-start(bf16[128,8,2048]{2,1,0:T(8,128)(2,1)} %convert_bitcast_fusion), calls=%async_computation.3 | async-start | bytes 8388608 | tf_op jit(solution)/shard_map/all_to_all | solution.py:227
  195.8 42.9 %copy-start.11 = (f32[64,128]{1,0:T(8,128)S(1)}, f32[64,128]{1,0:T(8,128)}, u32[]{:S(2)}) copy-start(f32[64,128]{1,0:T(8,128)} %copy-done.10) | copy-start | bytes 98308
  195.8 42.9 %copy-start.12 = (f32[64,128]{1,0:T(8,128)S(1)}, f32[64,128]{1,0:T(8,128)}, u32[]{:S(2)}) copy-start(f32[64,128]{1,0:T(8,128)} %get-tuple-element.6) | copy-start | bytes 98308
  232.9 58.5 %all-to-all-start.1 = ((bf16[128,8,2048]{2,1,0:T(8,128)(2,1)}), bf16[128,8,2048]{2,1,0:T(8,128)(2,1)}, u32[]{:S(2)}, u32[]{:S(2)}) async-start(bf16[128,8,2048]{2,1,0:T(8,128)(2,1)} %convert_bitcast_fusion.2), calls=%async_computation.1 | async-start | bytes 8388608 | tf_op jit(solution)/shard_map/all_to_all | solution.py:227
  291.5 5.1 %copy-start.6 = (bf16[128,2048]{1,0:T(8,128)(2,1)S(1)}, bf16[128,2048]{1,0:T(8,128)(2,1)}, u32[]{:S(2)}) copy-start(bf16[128,2048]{1,0:T(8,128)(2,1)} %copy-done.5) | copy-start | bytes 1572868

commit v4 on v1

--- a/solution.py
+++ b/solution.py
@@ -189,11 +189,116 @@
     )(q, k, v, sk, sv, tok, gain, ow)
 
 
-def half_expert(rows, gate_up, down_proj):
-    hidden_units = down_proj.shape[0]
-    projected = jnp.dot(rows, gate_up, preferred_element_type=F32)
-    active = (jax.nn.silu(projected[:, :hidden_units]) * projected[:, hidden_units:]).astype(BF16)
-    return jnp.dot(active, down_proj, preferred_element_type=F32).astype(BF16)
+def experts_kernel(
+    out_ref, gu_hbm, down_hbm, flat_ref,
+    recv, part, gu, down, proj, act,
+    recv_sem, send_sem, weight_sem,
+):
+    me = lax.axis_index("grp") * 32 + lax.axis_index("dev")
+    gu_copy = pltpu.make_async_copy(gu_hbm, gu, weight_sem.at[0])
+    down_copy = pltpu.make_async_copy(down_hbm, down, weight_sem.at[1])
+    gu_copy.start()
+    down_copy.start()
+
+    def place(i):
+        return {"grp": i // 32, "dev": i % 32}
+
+    barrier = pltpu.get_barrier_semaphore()
+
+    def greet(j, c):
+        pl.semaphore_signal(barrier, inc=1, device_id=place((me + j) % 128), device_id_type=MESH)
+        return c
+
+    lax.fori_loop(1, 128, greet, 0)
+    pl.semaphore_wait(barrier, 127)
+
+    pltpu.make_async_copy(out_ref.at[me // 2], recv.at[0], recv_sem.at[0]).start()
+
+    def send(j, c):
+        to = (me + j) % 128
+        pltpu.make_async_remote_copy(
+            out_ref.at[to // 2], recv.at[j], send_sem.at[0], recv_sem.at[j // 16],
+            device_id=place(to), device_id_type=MESH,
+        ).start()
+        return c
+
+    lax.fori_loop(1, 128, send, 0)
+    gu_copy.wait()
+    down_copy.wait()
+
+    def compute(g):
+        block = pl.ds(g * 16, 16)
+        pltpu.make_async_copy(recv.at[block], recv.at[block], recv_sem.at[g]).wait()
+        rows = recv[block].reshape(256, 2048)
+
+        def project(n, c):
+            cols = pl.ds(pl.multiple_of(n * 256, 256), 256)
+            proj[:, cols] = jnp.dot(rows, gu[:, cols], preferred_element_type=F32)
+            return c
+
+        lax.fori_loop(0, 5, project, 0)
+        proj[:, 1280:1408] = jnp.dot(rows, gu[:, 1280:1408], preferred_element_type=F32)
+        whole = proj[...]
+        up = pltpu.roll(whole, 704, 1)
+        gate = whole[:, :768]
+        act[...] = (gate / (1.0 + jnp.exp(-gate)) * up[:, :768]).astype(BF16)
+        hidden = act[:, :704]
+
+        def lower(n, c):
+            cols = pl.ds(pl.multiple_of(n * 512, 512), 512)
+            done = jnp.dot(hidden, down[:, cols], preferred_element_type=F32).astype(BF16)
+            part[block, :, cols] = done.reshape(16, 16, 512)
+            return c
+
+        lax.fori_loop(0, 4, lower, 0)
+
+    def give_back(j, c):
+        pltpu.make_async_remote_copy(
+            part.at[j], flat_ref.at[me], send_sem.at[1], recv_sem.at[8],
+            device_id=place((me + 128 - j) % 128), device_id_type=MESH,
+        ).start()
+        return c
+
+    compute(0)
+    pltpu.make_async_copy(part.at[0], flat_ref.at[me], recv_sem.at[8]).start()
+    lax.fori_loop(1, 16, give_back, 0)
+
+    def group(g, c):
+        compute(g)
+        lax.fori_loop(g * 16, g * 16 + 16, give_back, 0)
+        return c
+
+    lax.fori_loop(1, 8, group, 0)
+    sent = pl.ds(0, 127)
+    pltpu.make_async_copy(recv.at[sent], recv.at[sent], send_sem.at[0]).wait()
+    pltpu.make_async_copy(part.at[sent], part.at[sent], send_sem.at[1]).wait()
+    pltpu.make_async_copy(flat_ref, flat_ref, recv_sem.at[8]).wait()
+
+
+def expert_rows(outgoing, gate_up, down):
+    vmem = pl.BlockSpec(memory_space=pltpu.VMEM)
+    hbm = pl.BlockSpec(memory_space=pl.ANY)
+    return pl.pallas_call(
+        experts_kernel,
+        out_shape=jax.ShapeDtypeStruct((128, 16, 2048), BF16),
+        in_specs=[vmem, hbm, hbm],
+        out_specs=vmem,
+        scratch_shapes=[
+            pltpu.VMEM((128, 16, 2048), BF16),
+            pltpu.VMEM((128, 16, 2048), BF16),
+            pltpu.VMEM((2048, 1408), BF16),
+            pltpu.VMEM((704, 2048), BF16),
+            pltpu.VMEM((256, 1408), F32),
+            pltpu.VMEM((256, 768), BF16),
+            pltpu.SemaphoreType.DMA((9,)),
+            pltpu.SemaphoreType.DMA((2,)),
+            pltpu.SemaphoreType.DMA((2,)),
+        ],
+        compiler_params=pltpu.CompilerParams(
+            collective_id=1, has_side_effects=True, vmem_limit_bytes=56 * 1024 * 1024
+        ),
+        name="experts",
+    )(outgoing, gate_up, down)
 
 
 def on_device(
@@ -208,33 +313,25 @@
     before = (jnp.arange(rows_here)[:, None] < jnp.arange(rows_here)[None, :]).astype(BF16)
     rank = jnp.dot(member.astype(BF16), before, preferred_element_type=F32)
     position = jnp.where(member > 0, rank, -1.0)
-    place = position[:, None, :] == jnp.arange(capacity, dtype=F32)[None, :, None]
+    slot = jnp.arange(capacity, dtype=F32)
+    place = position[:, None, :] == slot[None, :, None]
     selected = place.astype(BF16).reshape(experts * capacity, rows_here)
     weights = jnp.where(place, gate[:, None, :], 0.0)
     high = weights.astype(BF16)
     low = (weights - high.astype(F32)).astype(BF16)
-    both = jnp.stack([high, low])[:, :, None]
-    both = jnp.broadcast_to(both, (2, experts, 2, capacity, rows_here)).reshape(2, 2 * experts * capacity, rows_here)
+    both = jnp.concatenate([high, low], axis=2)[:, None]
+    both = jnp.broadcast_to(both, (experts, 2, capacity, 2 * rows_here)).reshape(-1, 2 * rows_here)
 
     attended, normed = attention(
         queries, prefix_keys[0], prefix_values[0], suffix_keys, suffix_values, tokens,
         norm_gain.reshape(1, width), out_weight,
     )
     outgoing = jnp.dot(selected, normed, preferred_element_type=F32).astype(BF16)
-    buffer = jnp.broadcast_to(
-        outgoing.reshape(experts, 1, capacity, width), (experts, 2, capacity, width)
-    ).reshape(2 * experts, capacity, width)
-    received = lax.all_to_all(buffer, ("grp", "dev"), split_axis=0, concat_axis=0, tiled=True)
-    partial_rows = half_expert(
-        received.reshape(-1, width), gate_up_weight[0], down_weight[0]
-    ).reshape(2 * experts, capacity, width)
-    returned = lax.all_to_all(partial_rows, ("grp", "dev"), split_axis=0, concat_axis=0, tiled=True)
-    flat = returned.reshape(-1, width)
-    contract = (((0,), (0,)), ((), ()))
-    routed = lax.dot_general(both[0], flat, contract, preferred_element_type=F32) + lax.dot_general(
-        both[1], flat, contract, preferred_element_type=F32
+    flat = expert_rows(outgoing.reshape(experts, capacity, width), gate_up_weight[0], down_weight[0])
+    parts = lax.dot_general(
+        both, flat.reshape(-1, width), (((0,), (0,)), ((), ())), preferred_element_type=F32
     )
-    return (attended, routed.astype(BF16))
+    return (attended, (parts[:rows_here] + parts[rows_here:]).astype(BF16))
 
 
 def solution(mesh):

time: 327 us -> 298 us (0.911); the launches traced: 325 us -> 292 us
  Pallas kernels: 40.7 us -> 272 us
  blocking collectives: 107 us -> 0 us
  waiting for transfers between devices: 106 us -> 0 us
  matrix products: 44.4 us -> 9.05 us
  local copies, waits for them, and re-layouts: 15.6 us -> 7.62 us
  starting transfers between devices: 7.56 us -> 0 us
    pallas_call x0 -> x1, Pallas kernels: none -> 232 us  [expert_rows(): pl.pallas_call(experts_kernel, out_shape=jax.ShapeDtypeStruct((128, 16, 2...]
    all_to_all x1 -> x0, blocking collectives: 107 us -> none  [on_device(): lax.all_to_all(buffer, ('grp', 'dev'), split_axis=0, concat_axis=0, tiled...]
    all_to_all x1 -> x0, waiting for transfers between devices: 106 us -> none  [on_device(): lax.all_to_all(partial_rows, ('grp', 'dev'), split_axis=0, concat_axis=0,...]
    dot_general x4 -> x1, matrix products: 41.1 us -> 5.73 us  [on_device(): lax.dot_general(both, flat.reshape(-1, width), (((0,), (0,)), ((), ())),...]
    broadcast_in_dim x3 -> x1, local copies, waits for them, and re-layouts: 8 us -> 0.08 us  [on_device(): jnp.broadcast_to(both, (experts, 2, capacity, 2 * rows_here))]
    all_to_all x1 -> x0, starting transfers between devices: 7.56 us -> none  [on_device(): lax.all_to_all(partial_rows, ('grp', 'dev'), split_axis=0, concat_axis=0,...]
    unnamed x23 -> x15, local copies, waits for them, and re-layouts: 7.48 us -> 7.46 us
  transfers between devices with their start and end apart: 1 -> 0, of which waited for: 1 -> 0; matrix products, arithmetic and copies ran while one was open for 0% -> 0% of each run, Pallas kernels for 0% -> 0%
where the time goes in v4:
time: 298 us; the launch traced here: 292 us
  Pallas kernels  272 us (91%)
  matrix products  9.05 us (3%)
  local copies, waits for them, and re-layouts  7.62 us (3%)
    pallas_call x1, Pallas kernels, expert_rows(): pl.pallas_call(experts_kernel, out_shape=jax.ShapeDtypeStruct((128, 16, 2...  232 us
    pallas_call x1, Pallas kernels, attention(): pl.pallas_call(attention_kernel, out_shape=(jax.ShapeDtypeStruct((128, 20...  40.7 us
    unnamed x15, local copies, waits for them, and re-layouts  7.46 us

profile of v4, /device:TPU:1, one launch (start us, length us, event | category | flops | bytes accessed | tf_op | source)
XLA Modules:
  0.0 292.0 jit_solution(6106731518172796290)
XLA Ops:
  0.6 0.1 eq.45
  0.7 0.7 convert_reduce_fusion
  1.5 0.1 convolution_select_fusion
  1.6 0.2 bitcast_compare_fusion
  1.8 0.1 fusion.1
  1.9 0.1 select_convert_fusion
  2.0 0.1 pad_maximum_fusion
  2.1 0.1 broadcast_in_dim.47
  2.2 0.0 copy-start
  2.2 1.0 copy-done
  3.2 0.0 copy-start.1
  3.2 1.0 copy-done.1
  4.3 0.0 copy-start.2
  4.3 1.0 copy-done.2
  5.3 1.0 copy-done.3
  6.3 0.9 copy-done.4
  7.2 0.9 copy-done.5
  8.2 0.7 copy-done.6
  8.8 40.7 %attention.1 = (bf16[128,2048]{1,0:T(8,128)(2,1)S(1)}, bf16[128,2048]{1,0:T(8,128)(2,1)S(1)}) custom-call(bf16[128,2048]{1,0:T(8,128)(2,1)S(1)} %copy-done, bf16[32,2048]{1,0:T(8,128)(2,1)S(1)} %bitcast.16, bf16[32,2048]{1,0:T(8,128)(2,1)S(1)} %bitcast.17, bf16[128,2048]{1,0:T(8,128)(2,1)S(1)} %copy-done.1, bf16[128,2048]{1,0:T(8,128)(2,1)S(1)} %copy-done.2, ...), custom_call_target="tpu_custom_call" | custom-call | tf_op jit(solution)/shard_map/attention/pallas_call | solution.py:162
  49.5 3.2 %convolution_convert_fusion = bf16[1024,2048]{1,0:T(8,128)(2,1)} fusion(pred[1024,128]{1,0:T(32,128)(4,1)S(1)} %bitcast_compare_fusion, bf16[128,2048]{1,0:T(8,128)(2,1)S(1)} %get-tuple-element.5), kind=kOutput, calls=%fused_computation | convolution fusion | flops 538968064 | bytes 4849664 | tf_op jit(solution)/shard_map/dot_general | solution.py:329
  52.7 231.8 %experts.1 = bf16[128,16,2048]{2,1,0:T(8,128)(2,1)} custom-call(bf16[64,16,2048]{2,1,0:T(8,128)(2,1)} %bitcast.20, bf16[2048,1408]{1,0:T(8,128)(2,1)} %bitcast.22, bf16[704,2048]{1,0:T(8,128)(2,1)} %bitcast.23), custom_call_target="tpu_custom_call" | custom-call | tf_op jit(solution)/shard_map/experts/pallas_call | solution.py:281
  284.5 5.7 %fusion.3 = f32[256,2048]{1,0:T(8,128)S(1)} fusion(bf16[2048,256]{1,0:T(8,128)(2,1)S(1)} %bitcast.21, bf16[2048,2048]{1,0:T(8,128)(2,1)} %bitcast.19), kind=kOutput, calls=%fused_computation.15 | convolution fusion | flops 2147483648 | bytes 11534336 | tf_op jit(solution)/shard_map/dot_general | solution.py:331
  290.3 0.9 fusion
  291.2 0.8 copy.17
  (5 shorter events, 0.0 us)
Async XLA Ops:
  2.2 1.0 copy-start
  3.2 1.0 copy-start.1
  4.3 1.0 copy-start.2
  5.3 1.0 copy-start.3
  6.3 0.9 copy-start.4
  7.2 0.9 copy-start.5
  8.1 0.7 copy-start.6

commit v5 on v4

--- a/solution.py
+++ b/solution.py
@@ -191,10 +191,13 @@
 
 def experts_kernel(
     out_ref, gu_hbm, down_hbm, flat_ref,
-    recv, part, gu, down, proj, act,
-    recv_sem, send_sem, weight_sem,
+    recv, part, got, gu, down, proj, act,
+    direct_sem, relay_sem, got_sem, back_sem, send_sem, weight_sem,
 ):
     me = lax.axis_index("grp") * 32 + lax.axis_index("dev")
+    k = me // 2
+    x = me % 4
+    outer = ((x + 1) // 2 + 1) % 2
     gu_copy = pltpu.make_async_copy(gu_hbm, gu, weight_sem.at[0])
     down_copy = pltpu.make_async_copy(down_hbm, down, weight_sem.at[1])
     gu_copy.start()
@@ -203,33 +206,49 @@
     def place(i):
         return {"grp": i // 32, "dev": i % 32}
 
+    def member(q):
+        return place(4 * (q // 2) + outer * 3 * (q % 2) + (1 - outer) * (1 + q % 2))
+
+    partner = place(me + 1 - 2 * (me % 2))
+
     barrier = pltpu.get_barrier_semaphore()
+    pl.semaphore_signal(barrier, inc=1, device_id=partner, device_id_type=MESH)
 
     def greet(j, c):
-        pl.semaphore_signal(barrier, inc=1, device_id=place((me + j) % 128), device_id_type=MESH)
-        return c
-
-    lax.fori_loop(1, 128, greet, 0)
-    pl.semaphore_wait(barrier, 127)
-
-    pltpu.make_async_copy(out_ref.at[me // 2], recv.at[0], recv_sem.at[0]).start()
+        pl.semaphore_signal(barrier, inc=1, device_id=member((k + j) % 64), device_id_type=MESH)
+        return c
+
+    lax.fori_loop(1, 64, greet, 0)
+    pl.semaphore_wait(barrier, 64)
+
+    pltpu.make_async_copy(out_ref.at[k], recv.at[0, 0], direct_sem.at[0]).start()
 
     def send(j, c):
-        to = (me + j) % 128
-        pltpu.make_async_remote_copy(
-            out_ref.at[to // 2], recv.at[j], send_sem.at[0], recv_sem.at[j // 16],
-            device_id=place(to), device_id_type=MESH,
-        ).start()
-        return c
-
-    lax.fori_loop(1, 128, send, 0)
+        to = (k + j) % 64
+        pltpu.make_async_remote_copy(
+            out_ref.at[to], recv.at[j // 8, j % 8], send_sem.at[0], direct_sem.at[j // 8],
+            device_id=member(to), device_id_type=MESH,
+        ).start()
+        return c
+
+    lax.fori_loop(1, 64, send, 0)
+    own, other = pl.ds(0, 8), pl.ds(8, 8)
+
+    def relay(g):
+        pltpu.make_async_copy(recv.at[g, own], recv.at[g, own], direct_sem.at[g]).wait()
+        pltpu.make_async_remote_copy(
+            recv.at[g, own], recv.at[g, other], send_sem.at[1], relay_sem.at[g],
+            device_id=partner, device_id_type=MESH,
+        ).start()
+
+    relay(0)
+    relay(1)
     gu_copy.wait()
     down_copy.wait()
 
     def compute(g):
-        block = pl.ds(g * 16, 16)
-        pltpu.make_async_copy(recv.at[block], recv.at[block], recv_sem.at[g]).wait()
-        rows = recv[block].reshape(256, 2048)
+        pltpu.make_async_copy(recv.at[g, other], recv.at[g, other], relay_sem.at[g]).wait()
+        rows = recv[g].reshape(256, 2048)
 
         def project(n, c):
             cols = pl.ds(pl.multiple_of(n * 256, 256), 256)
@@ -247,32 +266,62 @@
         def lower(n, c):
             cols = pl.ds(pl.multiple_of(n * 512, 512), 512)
             done = jnp.dot(hidden, down[:, cols], preferred_element_type=F32).astype(BF16)
-            part[block, :, cols] = done.reshape(16, 16, 512)
+            part[g, :, :, cols] = done.reshape(16, 16, 512)
             return c
 
         lax.fori_loop(0, 4, lower, 0)
+        pltpu.make_async_remote_copy(
+            part.at[g, other], got.at[g], send_sem.at[2], got_sem.at[g],
+            device_id=partner, device_id_type=MESH,
+        ).start()
+
+    def finish(g):
+        pltpu.make_async_copy(got.at[g], got.at[g], got_sem.at[g]).wait()
+
+        def add(b, c):
+            part[g, b] = (part[g, b].astype(F32) + got[g, b].astype(F32)).astype(BF16)
+            return c
+
+        lax.fori_loop(0, 8, add, 0)
 
     def give_back(j, c):
         pltpu.make_async_remote_copy(
-            part.at[j], flat_ref.at[me], send_sem.at[1], recv_sem.at[8],
-            device_id=place((me + 128 - j) % 128), device_id_type=MESH,
-        ).start()
-        return c
-
-    compute(0)
-    pltpu.make_async_copy(part.at[0], flat_ref.at[me], recv_sem.at[8]).start()
-    lax.fori_loop(1, 16, give_back, 0)
+            part.at[j // 8, j % 8], flat_ref.at[k], send_sem.at[3], back_sem,
+            device_id=member((k + 64 - j) % 64), device_id_type=MESH,
+        ).start()
+        return c
 
     def group(g, c):
+        @pl.when(g < 6)
+        def _():
+            relay(g + 2)
+
         compute(g)
-        lax.fori_loop(g * 16, g * 16 + 16, give_back, 0)
-        return c
-
-    lax.fori_loop(1, 8, group, 0)
-    sent = pl.ds(0, 127)
-    pltpu.make_async_copy(recv.at[sent], recv.at[sent], send_sem.at[0]).wait()
-    pltpu.make_async_copy(part.at[sent], part.at[sent], send_sem.at[1]).wait()
-    pltpu.make_async_copy(flat_ref, flat_ref, recv_sem.at[8]).wait()
+
+        @pl.when(g == 2)
+        def _():
+            finish(0)
+            pltpu.make_async_copy(part.at[0, 0], flat_ref.at[k], back_sem).start()
+            lax.fori_loop(1, 8, give_back, 0)
+
+        @pl.when(g > 2)
+        def _():
+            finish(g - 2)
+            lax.fori_loop((g - 2) * 8, (g - 2) * 8 + 8, give_back, 0)
+
+        return c
+
+    lax.fori_loop(0, 8, group, 0)
+    finish(6)
+    lax.fori_loop(48, 56, give_back, 0)
+    finish(7)
+    lax.fori_loop(56, 64, give_back, 0)
+    left = flat_ref.at[pl.ds(0, 63)]
+    pltpu.make_async_copy(left, left, send_sem.at[0]).wait()
+    pltpu.make_async_copy(flat_ref, flat_ref, send_sem.at[1]).wait()
+    pltpu.make_async_copy(flat_ref, flat_ref, send_sem.at[2]).wait()
+    pltpu.make_async_copy(left, left, send_sem.at[3]).wait()
+    pltpu.make_async_copy(flat_ref, flat_ref, back_sem).wait()
 
 
 def expert_rows(outgoing, gate_up, down):
@@ -280,18 +329,22 @@
     hbm = pl.BlockSpec(memory_space=pl.ANY)
     return pl.pallas_call(
         experts_kernel,
-        out_shape=jax.ShapeDtypeStruct((128, 16, 2048), BF16),
+        out_shape=jax.ShapeDtypeStruct((64, 16, 2048), BF16),
         in_specs=[vmem, hbm, hbm],
         out_specs=vmem,
         scratch_shapes=[
-            pltpu.VMEM((128, 16, 2048), BF16),
-            pltpu.VMEM((128, 16, 2048), BF16),
+            pltpu.VMEM((8, 16, 16, 2048), BF16),
+            pltpu.VMEM((8, 16, 16, 2048), BF16),
+            pltpu.VMEM((8, 8, 16, 2048), BF16),
             pltpu.VMEM((2048, 1408), BF16),
             pltpu.VMEM((704, 2048), BF16),
             pltpu.VMEM((256, 1408), F32),
             pltpu.VMEM((256, 768), BF16),
-            pltpu.SemaphoreType.DMA((9,)),
-            pltpu.SemaphoreType.DMA((2,)),
+            pltpu.SemaphoreType.DMA((8,)),
+            pltpu.SemaphoreType.DMA((8,)),
+            pltpu.SemaphoreType.DMA((8,)),
+            pltpu.SemaphoreType.DMA,
+            pltpu.SemaphoreType.DMA((4,)),
             pltpu.SemaphoreType.DMA((2,)),
         ],
         compiler_params=pltpu.CompilerParams(
@@ -319,8 +372,7 @@
     weights = jnp.where(place, gate[:, None, :], 0.0)
     high = weights.astype(BF16)
     low = (weights - high.astype(F32)).astype(BF16)
-    both = jnp.concatenate([high, low], axis=2)[:, None]
-    both = jnp.broadcast_to(both, (experts, 2, capacity, 2 * rows_here)).reshape(-1, 2 * rows_here)
+    both = jnp.concatenate([high, low], axis=2).reshape(experts * capacity, 2 * rows_here)
 
     attended, normed = attention(
         queries, prefix_keys[0], prefix_values[0], suffix_keys, suffix_values, tokens,

time: 298 us -> 281 us (0.943)
  Pallas kernels: 272 us -> 258 us
    pallas_call x1, Pallas kernels: 232 us -> 217 us  [expert_rows(): pl.pallas_call(experts_kernel, out_shape=jax.ShapeDtypeStruct((64, 16, 20...]
    unnamed x15 -> x19, local copies, waits for them, and re-layouts: 7.46 us -> 7.46 us
where the time goes in v5:
time: 281 us; the launch traced here: 278 us
  Pallas kernels  258 us (92%)
  matrix products  10.5 us (4%)
  local copies, waits for them, and re-layouts  7.55 us (3%)
    pallas_call x1, Pallas kernels, expert_rows(): pl.pallas_call(experts_kernel, out_shape=jax.ShapeDtypeStruct((64, 16, 20...  217 us
    pallas_call x1, Pallas kernels, attention(): pl.pallas_call(attention_kernel, out_shape=(jax.ShapeDtypeStruct((128, 20...  40.9 us
    unnamed x19, local copies, waits for them, and re-layouts  7.46 us
    dot_general x1, matrix products, on_device(): lax.dot_general(both, flat.reshape(-1, width), (((0,), (0,)), ((), ())),...  7.14 us

profile of v5, /device:TPU:1, one launch (start us, length us, event | category | flops | bytes accessed | tf_op | source)
XLA Modules:
  0.0 277.8 jit_solution(12686717174896010231)
XLA Ops:
  0.6 0.0 copy-start
  0.6 1.0 copy-done
  1.7 0.0 copy-start.1
  1.7 1.0 copy-done.1
  2.7 0.0 copy-start.2
  2.7 1.0 copy-done.2
  3.8 0.0 copy-start.3
  3.8 1.0 copy-done.3
  4.8 0.9 copy-done.4
  5.7 0.9 copy-done.5
  6.6 0.7 copy-done.6
  7.3 40.9 %attention.1 = (bf16[128,2048]{1,0:T(8,128)(2,1)S(1)}, bf16[128,2048]{1,0:T(8,128)(2,1)S(1)}) custom-call(bf16[128,2048]{1,0:T(8,128)(2,1)S(1)} %copy-done, bf16[32,2048]{1,0:T(8,128)(2,1)S(1)} %bitcast.14, bf16[32,2048]{1,0:T(8,128)(2,1)S(1)} %bitcast.15, bf16[128,2048]{1,0:T(8,128)(2,1)S(1)} %copy-done.1, bf16[128,2048]{1,0:T(8,128)(2,1)S(1)} %copy-done.2, ...), custom_call_target="tpu_custom_call" | custom-call | tf_op jit(solution)/shard_map/attention/pallas_call | solution.py:162
  48.2 0.0 copy-done.7
  48.2 0.0 copy-done.8
  48.3 0.1 convolution_select_fusion
  48.4 0.1 eq.45
  48.5 0.2 bitcast_compare_fusion
  48.7 3.2 %convolution_convert_fusion = bf16[1024,2048]{1,0:T(8,128)(2,1)} fusion(pred[1024,128]{1,0:T(32,128)(4,1)S(1)} %bitcast_compare_fusion, bf16[128,2048]{1,0:T(8,128)(2,1)S(1)} %get-tuple-element.5), kind=kOutput, calls=%fused_computation.2 | convolution fusion | flops 538968064 | bytes 4849664 | tf_op jit(solution)/shard_map/dot_general | solution.py:381
  51.9 216.9 %experts.1 = bf16[64,16,2048]{2,1,0:T(8,128)(2,1)} custom-call(bf16[64,16,2048]{2,1,0:T(8,128)(2,1)} %bitcast.17, bf16[2048,1408]{1,0:T(8,128)(2,1)} %bitcast.18, bf16[704,2048]{1,0:T(8,128)(2,1)} %bitcast.19), custom_call_target="tpu_custom_call" | custom-call | tf_op jit(solution)/shard_map/experts/pallas_call | solution.py:330
  268.8 0.1 fusion.6
  268.9 0.1 select_convert_fusion
  269.0 7.1 %fusion.2 = f32[256,2048]{1,0:T(8,128)S(1)} fusion(bf16[64,16,2048]{2,1,0:T(8,128)(2,1)} %experts.1, bf16[64,16,128]{2,0,1:T(8,128)(2,1)S(1)} %fusion.6, bf16[64,16,128]{2,0,1:T(8,128)(2,1)S(1)} %select_convert_fusion), kind=kOutput, calls=%fused_computation.3 | convolution fusion | flops 1074790400 | bytes 6815744 | tf_op jit(solution)/shard_map/dot_general | solution.py:383
  276.1 0.9 fusion.5
  277.0 0.8 copy.27
  (7 shorter events, 0.1 us)
Async XLA Ops:
  0.6 1.0 copy-start
  1.7 1.0 copy-start.1
  2.7 1.0 copy-start.2
  3.8 1.0 copy-start.3
  4.8 0.9 copy-start.4
  5.7 0.9 copy-start.5
  6.6 0.7 copy-start.6
  7.3 40.9 %copy-start.7 = (f32[128,6]{0,1:T(8,128)S(1)}, f32[128,6]{0,1:T(8,128)}, u32[]{:S(2)}) copy-start(f32[128,6]{0,1:T(8,128)} %param.21) | copy-start | bytes 9220
  7.3 40.9 %copy-start.8 = (s32[128,6]{0,1:T(8,128)S(1)}, s32[128,6]{0,1:T(8,128)}, u32[]{:S(2)}) copy-start(s32[128,6]{0,1:T(8,128)} %param.20) | copy-start | bytes 9220

commit v6 on v5

--- a/solution.py
+++ b/solution.py
@@ -18,10 +18,11 @@
 
 
 def attention_kernel(
-    q_ref, k_ref, v_ref, sk_ref, sv_ref, tok_ref, gain_ref, ow_hbm,
+    q_hbm, k_hbm, v_hbm, sk_hbm, sv_hbm, tok_hbm, gain_ref, ow_hbm,
     attended_ref, normed_ref,
     qbuf, kbuf, vbuf, osend, orecv, stsend, strecv, suf_acc, suf_stat, vt, hout, resid, ow,
-    recv_sem, send_sem, ow_sem,
+    q_ref, k_ref, v_ref, sk_ref, sv_ref, tok_ref,
+    recv_sem, send_sem, ow_sem, in_sem,
 ):
     me = lax.axis_index("dev")
     y, zh, x = me // 8, (me // 4) % 2, me % 4
@@ -29,6 +30,10 @@
     scale = 1.0 / math.sqrt(HEAD_DIM)
 
     ow_copy = pltpu.make_async_copy(ow_hbm, ow, ow_sem)
+    pairs = ((k_hbm, k_ref), (v_hbm, v_ref), (q_hbm, q_ref), (sk_hbm, sk_ref), (sv_hbm, sv_ref), (tok_hbm, tok_ref))
+    loads = [pltpu.make_async_copy(src, dst, in_sem.at[n]) for n, (src, dst) in enumerate(pairs)]
+    for load in loads:
+        load.start()
     ow_copy.start()
 
     barrier = pltpu.get_barrier_semaphore()
@@ -45,6 +50,9 @@
 
     def key_rows(d):
         return pl.ds(pl.multiple_of(d * 32, 32), 32)
+
+    for load in loads[:3]:
+        load.wait()
 
     pltpu.make_async_copy(q_ref.at[:, columns(head)], qbuf.at[head], recv_sem.at[0]).start()
     pltpu.make_async_copy(k_ref.at[:, columns(head)], kbuf.at[key_rows(me), :], recv_sem.at[1]).start()
@@ -80,6 +88,8 @@
     key_at = lax.broadcasted_iota(jnp.int32, (128, 128), 0)
     query_at = lax.broadcasted_iota(jnp.int32, (128, 128), 1)
     allowed = key_at <= query_at
+    for load in loads[3:]:
+        load.wait()
     for h in range(HEADS):
         cols = slice(h * HEAD_DIM, (h + 1) * HEAD_DIM)
         s = lax.dot_general(sk_ref[:, cols], q_ref[:, cols], NT, preferred_element_type=F32) * scale
@@ -162,7 +172,7 @@
     return pl.pallas_call(
         attention_kernel,
         out_shape=(jax.ShapeDtypeStruct((128, 2048), BF16), jax.ShapeDtypeStruct((128, 2048), BF16)),
-        in_specs=[vmem] * 7 + [pl.BlockSpec(memory_space=pl.ANY)],
+        in_specs=[pl.BlockSpec(memory_space=pltpu.HBM)] * 6 + [vmem, pl.BlockSpec(memory_space=pltpu.HBM)],
         out_specs=(vmem, vmem),
         scratch_shapes=[
             pltpu.VMEM((16, 128, 128), BF16),
@@ -178,12 +188,19 @@
             pltpu.VMEM((128, 2048), BF16),
             pltpu.VMEM((128, 2048), F32),
             pltpu.VMEM((2048, 2048), BF16),
+            pltpu.VMEM((128, 2048), BF16),
+            pltpu.VMEM((32, 2048), BF16),
+            pltpu.VMEM((32, 2048), BF16),
+            pltpu.VMEM((128, 2048), BF16),
+            pltpu.VMEM((128, 2048), BF16),
+            pltpu.VMEM((128, 2048), BF16),
             pltpu.SemaphoreType.DMA((5,)),
             pltpu.SemaphoreType.DMA((5,)),
             pltpu.SemaphoreType.DMA,
+            pltpu.SemaphoreType.DMA((6,)),
         ],
         compiler_params=pltpu.CompilerParams(
-            collective_id=0, has_side_effects=True, vmem_limit_bytes=48 * 1024 * 1024
+            collective_id=0, has_side_effects=True, vmem_limit_bytes=67_043_328
         ),
         name="attention",
     )(q, k, v, sk, sv, tok, gain, ow)

time: 281 us -> 278 us (0.989)
  local copies, waits for them, and re-layouts: 7.55 us -> 0.88 us
    unnamed x19 -> x3, local copies, waits for them, and re-layouts: 7.46 us -> 0.8 us
where the time goes in v6:
time: 278 us; the launch traced here: 275 us
  Pallas kernels  260 us (94%)
  matrix products  11.5 us (4%)
    pallas_call x1, Pallas kernels, expert_rows(): pl.pallas_call(experts_kernel, out_shape=jax.ShapeDtypeStruct((64, 16, 20...  217 us
    pallas_call x1, Pallas kernels, attention(): pl.pallas_call(attention_kernel, out_shape=(jax.ShapeDtypeStruct((128, 20...  42.6 us
    dot_general x1, matrix products, on_device(): lax.dot_general(both, flat.reshape(-1, width), (((0,), (0,)), ((), ())),...  7.2 us

profile of v6, /device:TPU:1, one launch (start us, length us, event | category | flops | bytes accessed | tf_op | source)
XLA Modules:
  0.0 274.7 jit_solution(4256585848428283393)
XLA Ops:
  0.6 42.6 %attention.1 = (bf16[128,2048]{1,0:T(8,128)(2,1)}, bf16[128,2048]{1,0:T(8,128)(2,1)}) custom-call(bf16[128,2048]{1,0:T(8,128)(2,1)} %q_hbm.1, bf16[32,2048]{1,0:T(8,128)(2,1)} %bitcast.17, bf16[32,2048]{1,0:T(8,128)(2,1)} %bitcast.18, bf16[128,2048]{1,0:T(8,128)(2,1)} %sk_hbm.1, bf16[128,2048]{1,0:T(8,128)(2,1)} %sv_hbm.1, bf16[128,2048]{1,0:T(8,128)(2,1)} %tok_hbm.1, ...), custom_call_target="tpu_custom_call" | custom-call | tf_op jit(solution)/shard_map/attention/pallas_call | solution.py:172
  43.3 0.7 select_reduce_fusion
  44.0 0.1 convolution_select_fusion
  44.2 0.1 eq.45
  44.3 0.2 bitcast_compare_fusion
  44.5 4.2 %convolution_convert_fusion = bf16[1024,2048]{1,0:T(8,128)(2,1)} fusion(pred[1024,128]{1,0:T(32,128)(4,1)S(1)} %bitcast_compare_fusion, bf16[128,2048]{1,0:T(8,128)(2,1)} %get-tuple-element.5), kind=kOutput, calls=%fused_computation.2 | convolution fusion | flops 538968064 | bytes 4849664 | tf_op jit(solution)/shard_map/dot_general | solution.py:398
  48.7 216.9 %experts.1 = bf16[64,16,2048]{2,1,0:T(8,128)(2,1)} custom-call(bf16[64,16,2048]{2,1,0:T(8,128)(2,1)} %bitcast.14, bf16[2048,1408]{1,0:T(8,128)(2,1)} %bitcast.15, bf16[704,2048]{1,0:T(8,128)(2,1)} %bitcast.16), custom_call_target="tpu_custom_call" | custom-call | tf_op jit(solution)/shard_map/experts/pallas_call | solution.py:347
  265.6 0.1 fusion.6
  265.7 0.1 select_convert_fusion
  265.8 0.0 copy-start
  265.8 7.2 %fusion.2 = f32[256,2048]{1,0:T(8,128)S(1)} fusion(bf16[64,16,2048]{2,1,0:T(8,128)(2,1)} %experts.1, bf16[64,16,128]{2,0,1:T(8,128)(2,1)S(1)} %fusion.6, bf16[64,16,128]{2,0,1:T(8,128)(2,1)S(1)} %select_convert_fusion), kind=kOutput, calls=%fused_computation.3 | convolution fusion | flops 1074790400 | bytes 6815744 | tf_op jit(solution)/shard_map/dot_general | solution.py:400
  273.0 0.9 fusion.5
  273.9 0.0 copy-done
  273.9 0.8 copy.27
  (1 shorter events, 0.0 us)
Async XLA Ops:
  265.8 8.1 %copy-start = (bf16[128,2048]{1,0:T(8,128)(2,1)S(1)}, bf16[128,2048]{1,0:T(8,128)(2,1)}, u32[]{:S(2)}) copy-start(bf16[128,2048]{1,0:T(8,128)(2,1)} %get-tuple-element.10) | copy-start | bytes 1572868
